TPU v7x, 256 devices: a whole 4x4x8 slice. The times are simulated.
256 devices in a mesh: dp: 16 (over y, x), expert: 16 (over z, core).
Axes of the slice: x: 4, y: 4, z: 8, core: 2. Of those that a mesh axis runs over, the one named last changes fastest.
Arguments:
- tokens: bfloat16 [32768, 1024], P(('dp', 'expert')), may hold values from -24 to 24
- routes: int32 [32768, 8], P(('dp', 'expert')), may hold values from 0 to 63, all different within a row; in each aligned block of 128 rows (0 to 127, 128 to 255, ...) at most 24 rows name the same one
- gate_weights: float32 [32768, 8], P(('dp', 'expert')), may hold values from 0.05 to 0.25
- cotangent: bfloat16 [32768, 1024], P(('dp', 'expert')), may hold values from -24 to 24
- w_gate_up: bfloat16 [1024, 64, 768], P(None, 'expert'), may hold values from -0.1875 to 0.1875
- w_down: bfloat16 [1024, 64, 384], P(None, 'expert'), may hold values from -0.3125 to 0.3125
Outputs:
- layer_out: bfloat16 [32768, 1024], P(('dp', 'expert'))
- grad_tokens: bfloat16 [32768, 1024], P(('dp', 'expert'))
- grad_gate_up: bfloat16 [1024, 64, 768], P('dp', 'expert')
- grad_down: bfloat16 [1024, 64, 384], P('dp', 'expert')
Inputs may be any that keep to these rules, and one draw needn't show every extreme that they name: `routes`: each row names 8 different experts. Among the 128 rows of one device no expert is named more than 24 times, and in some device's rows an expert is named exactly 24 times.
All inputs are finite; a program needn't handle non-finite values.
Results may differ from a plain program's by a relative error of at most 0.015.
Values may be sent and summed in bfloat16 or wider, within the bound.
A program may use at most 128 MiB of HBM per device.

v0:
```python
import jax
import jax.numpy as jnp
from jax import lax
from jax.sharding import PartitionSpec as P


def split_parts(projected, hidden_units):
    gate_part = projected[..., :hidden_units]
    up_part = projected[..., hidden_units:]
    sigma = jax.nn.sigmoid(gate_part)
    return (gate_part, up_part, sigma)


def forward_local(received, w_gate_up, w_down, hidden_units):
    projected = jnp.einsum(
        "slmd,dlf->slmf", received, w_gate_up, preferred_element_type=jnp.float32
    )
    gate_part, up_part, sigma = split_parts(projected, hidden_units)
    hidden_fwd = (gate_part * sigma * up_part).astype(jnp.bfloat16)
    expert_out = jnp.einsum(
        "slmh,dlh->slmd", hidden_fwd, w_down, preferred_element_type=jnp.float32
    ).astype(jnp.bfloat16)
    return (projected, expert_out)


def backward_local(projected, received_cot, w_gate_up, w_down, hidden_units):
    gate_part, up_part, sigma = split_parts(projected, hidden_units)
    hidden = (gate_part * sigma * up_part).astype(jnp.bfloat16)
    d_hidden = jnp.einsum(
        "slmd,dlh->slmh", received_cot, w_down, preferred_element_type=jnp.float32
    )
    d_gate = d_hidden * up_part * sigma * (1.0 + gate_part * (1.0 - sigma))
    d_up = d_hidden * gate_part * sigma
    d_proj = jnp.concatenate([d_gate, d_up], axis=-1).astype(jnp.bfloat16)
    slot_grads = jnp.einsum(
        "slmf,dlf->slmd", d_proj, w_gate_up, preferred_element_type=jnp.float32
    ).astype(jnp.bfloat16)
    return (hidden, d_proj, slot_grads)


def per_device(tokens, routes, gate_weights, cotangent, w_gate_up, w_down):
    tok_dev, active = routes.shape
    model_width = tokens.shape[1]
    exp_dev = w_down.shape[1]
    hidden_units = w_down.shape[2]
    expert_peers = lax.axis_size("expert")
    experts_all = exp_dev * expert_peers
    capacity = 3 * tok_dev * active // (2 * experts_all)
    assigned = tok_dev * active
    slots_all = experts_all * capacity
    flat_routes = routes.reshape(assigned)
    onehot = (flat_routes[:, None] == jnp.arange(experts_all, dtype=jnp.int32)[None, :]).astype(
        jnp.int32
    )
    slot_rank = jnp.sum((jnp.cumsum(onehot, axis=0) - 1) * onehot, axis=1)
    slot_index = flat_routes * capacity + slot_rank
    source_of = (
        jnp.zeros((slots_all,), jnp.int32).at[slot_index].set(jnp.arange(assigned, dtype=jnp.int32))
    )
    filled = jnp.zeros((slots_all,), jnp.int32).at[slot_index].set(1) > 0
    token_of = source_of // active
    empty_row = jnp.zeros((), jnp.bfloat16)
    slot_shape = (expert_peers, exp_dev, capacity, model_width)
    x_slots = jnp.where(filled[:, None], tokens[token_of], empty_row).reshape(slot_shape)
    flat_gates = gate_weights.reshape(assigned)
    weighted = (flat_gates[source_of][:, None] * cotangent[token_of].astype(jnp.float32)).astype(
        jnp.bfloat16
    )
    cot_slots = jnp.where(filled[:, None], weighted, empty_row).reshape(slot_shape)
    expert_out = forward_local(
        lax.all_to_all(x_slots, "expert", split_axis=0, concat_axis=0, tiled=True),
        w_gate_up,
        w_down,
        hidden_units,
    )[1]
    returned = lax.all_to_all(expert_out, "expert", split_axis=0, concat_axis=0, tiled=True)
    received_x, received_cot = (
        lax.all_to_all(x_slots, "expert", split_axis=0, concat_axis=0, tiled=True),
        lax.all_to_all(cot_slots, "expert", split_axis=0, concat_axis=0, tiled=True),
    )
    projected = jnp.einsum(
        "slmd,dlf->slmf", received_x, w_gate_up, preferred_element_type=jnp.float32
    )
    hidden, d_proj, slot_grads = backward_local(
        projected, received_cot, w_gate_up, w_down, hidden_units
    )
    grad_back = lax.all_to_all(slot_grads, "expert", split_axis=0, concat_axis=0, tiled=True)
    per_assign = returned.reshape(slots_all, model_width)[slot_index].reshape(
        tok_dev, active, model_width
    )
    layer_out = jnp.sum(per_assign.astype(jnp.float32) * gate_weights[:, :, None], axis=1).astype(
        jnp.bfloat16
    )
    grad_assign = grad_back.reshape(slots_all, model_width)[slot_index].reshape(
        tok_dev, active, model_width
    )
    grad_tokens = jnp.sum(grad_assign.astype(jnp.float32), axis=1).astype(jnp.bfloat16)
    term_gu = jnp.einsum("slmd,slmf->dlf", received_x, d_proj, preferred_element_type=jnp.float32)
    term_dn = jnp.einsum("slmd,slmh->dlh", received_cot, hidden, preferred_element_type=jnp.float32)
    summed = lax.psum_scatter(
        jnp.concatenate([term_gu, term_dn], axis=2).astype(jnp.bfloat16),
        "dp",
        scatter_dimension=0,
        tiled=True,
    ).astype(jnp.float32)
    grad_gate_up = summed[:, :, : 2 * hidden_units].astype(jnp.bfloat16)
    grad_down = summed[:, :, 2 * hidden_units :].astype(jnp.bfloat16)
    return (layer_out, grad_tokens, grad_gate_up, grad_down)


def solution(mesh):
    in_specs = (
        P(("dp", "expert"), None),
        P(("dp", "expert"), None),
        P(("dp", "expert"), None),
        P(("dp", "expert"), None),
        P(None, "expert", None),
        P(None, "expert", None),
    )
    out_specs = (
        P(("dp", "expert"), None),
        P(("dp", "expert"), None),
        P("dp", "expert", None),
        P("dp", "expert", None),
    )
    return jax.shard_map(
        per_device, mesh=mesh, in_specs=in_specs, out_specs=out_specs, check_vma=False
    )
```

profile of v0, /device:TPU:1, one launch (start us, length us, event | category | flops | bytes accessed | tf_op | source)
XLA Modules:
  0.0 458.1 jit_solution(14948126099717946188)
XLA Ops:
  7.2 0.0 copy-start
  7.2 0.8 broadcast_multiply_fusion
  8.0 0.9 copy.37
  8.9 0.1 eq.29
  9.0 0.1 eq.25
  9.1 0.1 copy.36
  9.2 0.1 mul.66
  9.3 0.7 fusion.36
  10.0 31.1 %reduce-window.6 = s32[64,8,128]{2,1,0:T(8,128)S(1)} reduce-window(s32[64,8,128]{2,1,0:T(8,128)} %fusion.36, s32[]{:T(128)} %constant.13.clone.1), window={size=1x1x128 pad=0_0x0_0x127_0}, to_apply=%region_0.0 | reduce-window | flops 8323072 | bytes 524292 | tf_op jit(solution)/shard_map/reduce-window
  41.1 0.8 slice.38
  42.0 1.1 copy.39
  43.1 0.1 copy.40
  43.2 0.1 add_add_fusion
  43.3 0.1 fusion.35
  43.4 4.3 scatter_custom_fusion.1
  47.8 0.8 copy.45
  48.5 0.1 reshape.96
  48.6 0.0 copy-start.2
  48.7 5.9 %gather_fusion.2 = f32[1536]{0:T(1024)S(1)} fusion(f32[1024]{0:T(1024)S(1)} %reshape.96, s32[2048]{0:T(1024)S(1)} %get-tuple-element.19), kind=kCustom, calls=%fused_computation.2 | custom fusion | bytes 18432 | tf_op jit(solution)/shard_map/gather | solution.py:66
  54.5 0.1 mul.72
  54.6 4.3 scatter_custom_fusion
  59.0 0.1 broadcast_in_dim.38
  59.1 0.0 copy-done.2
  59.1 5.8 %gather_fusion.3 = bf16[1536,1024]{1,0:T(8,128)(2,1)} fusion(bf16[128,1024]{1,0:T(8,128)(2,1)S(1)} %copy-done.2, s32[2048]{0:T(1024)S(1)} %get-tuple-element.20), kind=kCustom, calls=%fused_computation.3 | custom fusion | bytes 6297600 | tf_op jit(solution)/shard_map/gather | solution.py:66
  64.9 8.8 %gather_fusion = bf16[1536,1024]{1,0:T(8,128)(2,1)} fusion(bf16[128,1024]{1,0:T(8,128)(2,1)} %param.6, s32[2048]{0:T(1024)S(1)} %get-tuple-element.20), kind=kCustom, calls=%fused_computation | custom fusion | bytes 6297600 | tf_op jit(solution)/shard_map/gather | solution.py:64
  73.7 4.8 %fusion.8 = (bf16[16,4,24,1024]{3,2,1,0:T(8,128)(2,1)}, bf16[16,4,24,1024]{3,2,1,0:T(8,128)(2,1)S(1)}) fusion(bf16[16,4,24,1024]{3,2,1,0:T(8,128)(2,1)} %bitcast.69, f32[16,4,24]{2,1,0:T(4,128)S(1)} %mul.72, pred[16,4,24]{2,1,0:T(4,128)(4,1)S(1)} %broadcast_in_dim.38, bf16[16,4,24,1024]{3,2,1,0:T(8,128)(2,1)} %bitcast.70), kind=kLoop, calls=%fused_computation.20 | loop fusion | flops 7864320 | bytes 12590592 | tf_op jit(solution)/shard_map/jit(_where)/select_n | solution.py:69
  78.5 83.4 %all_to_all.21 = bf16[16,4,24,1024]{3,2,1,0:T(8,128)(2,1)} all-to-all(bf16[16,4,24,1024]{3,2,1,0:T(8,128)(2,1)S(1)} %get-tuple-element.16), channel_id=1, replica_groups=mesh['dp'=16,'expert'=16] {'expert'}, dimensions={0} | all-to-all | bytes 6291456 | tf_op jit(solution)/shard_map/all_to_all | solution.py:71
  161.9 4.6 all-to-all-start.2
  166.5 8.6 %fusion.25 = f32[16,4,24,768]{3,2,0,1:T(8,128)} fusion(bf16[1024,4,768,1]{2,1,0,3:T(4,128)(2,1)} %bitcast.77, bf16[16,4,24,1024]{3,2,1,0:T(8,128)(2,1)} %all_to_all.21), kind=kOutput, calls=%fused_computation.43 | convolution fusion | flops 2415919104 | bytes 14155776 | tf_op jit(solution)/shard_map/slmd,dlf->slmf/dot_general | solution.py:15
  175.0 61.0 %all-to-all-done.2 = bf16[16,4,24,1024]{3,2,1,0:T(8,128)(2,1)} async-done(((bf16[16,4,24,1024]{3,2,1,0:T(8,128)(2,1)}), bf16[16,4,24,1024]{3,2,1,0:T(8,128)(2,1)}, u32[]{:S(2)}, u32[]{:S(2)}) %all-to-all-start.2) | async-done | bytes 3145760 | tf_op jit(solution)/shard_map/all_to_all | solution.py:79
  236.1 0.0 copy-done
  236.1 7.3 %fusion.20 = (bf16[16,4,24,384]{3,2,0,1:T(8,128)(2,1)}, bf16[16,4,24,384]{3,2,0,1:T(8,128)(2,1)}, bf16[16,4,24,384]{3,2,0,1:T(8,128)(2,1)S(1)}) fusion(f32[16,4,24,768]{3,2,0,1:T(8,128)} %fusion.25, bf16[1024,4,384,1]{2,1,0,3:T(4,128)(2,1)S(1)} %bitcast.67, bf16[16,4,24,1024]{3,2,1,0:T(8,128)(2,1)} %all-to-all-done.2), kind=kOutput, calls=%fused_computation.38 | convolution fusion | flops 1217396736 | bytes 14548992 | tf_op jit(solution)/shard_map/slmd,dlh->slmh/dot_general | solution.py:29
  243.4 0.0 copy-start.5
  243.4 1.9 convert_bitcast_fusion.1
  245.2 0.0 copy-done.5
  245.3 2.0 copy.44
  247.3 5.4 %all-to-all-start.1 = ((bf16[16,4,24,1024]{3,2,1,0:T(8,128)(2,1)}), bf16[16,4,24,1024]{3,2,1,0:T(8,128)(2,1)S(1)}, u32[]{:S(2)}, u32[]{:S(2)}) async-start(bf16[16,4,24,1024]{3,2,1,0:T(8,128)(2,1)} %copy.44), calls=%async_computation.1 | async-start | bytes 6291456 | tf_op jit(solution)/shard_map/all_to_all | solution.py:76
  252.7 0.3 all-reduce.3.cloned.1.call-start
  252.9 0.0 copy-start.6
  252.9 6.2 %fusion = bf16[1024,4,768]{0,2,1:T(8,128)(2,1)S(1)} fusion(bf16[16,4,24,1024]{3,2,1,0:T(8,128)(2,1)} %all_to_all.21, bf16[16,4,24,384]{3,2,0,1:T(8,128)(2,1)} %get-tuple-element.13, bf16[16,4,24,384]{3,2,0,1:T(8,128)(2,1)} %get-tuple-element.12), kind=kOutput, calls=%fused_computation.9 | convolution fusion | flops 2423783424 | bytes 11796480 | tf_op jit(solution)/shard_map/slmd,slmf->dlf/dot_general | solution.py:98
  259.1 0.0 copy-done.6
  259.1 3.7 fusion.7
  262.8 8.1 %pad_maximum_fusion = bf16[1024,4,1152]{0,2,1:T(8,128)(2,1)} fusion(bf16[1024,4,384]{0,2,1:T(8,128)(2,1)S(1)} %fusion.7, bf16[1024,4,768]{0,2,1:T(8,128)(2,1)S(1)} %fusion), kind=kLoop, calls=%fused_computation.8 | loop fusion | flops 18874368 | bytes 18874368 | tf_op jit(solution)/shard_map/concatenate | solution.py:101
  271.0 15.5 %copy.53 = bf16[1024,4,1152]{2,1,0:T(4,128)(2,1)} copy(bf16[1024,4,1152]{0,2,1:T(8,128)(2,1)} %pad_maximum_fusion) | data formatting | bytes 18874368 | tf_op jit(solution)/shard_map/concatenate | solution.py:101
  286.5 0.0 all-reduce.3.cloned.1.call-update
  286.5 6.2 %convert_bitcast_fusion = bf16[16,4,24,1024]{3,2,0,1:T(8,128)(2,1)S(1)} fusion(bf16[1024,4,768,1]{2,1,0,3:T(4,128)(2,1)} %bitcast.78, bf16[16,4,24,384]{3,2,0,1:T(8,128)(2,1)} %get-tuple-element.13, bf16[16,4,24,384]{3,2,0,1:T(8,128)(2,1)} %get-tuple-element.12), kind=kOutput, calls=%fused_computation.21 | convolution fusion | flops 2422210560 | bytes 11796480 | tf_op jit(solution)/shard_map/slmf,dlf->slmd/dot_general | solution.py:35
  292.6 2.0 copy.50
  294.6 0.0 copy-start.4
  294.6 29.1 %all-to-all-done.1 = bf16[16,4,24,1024]{3,2,1,0:T(8,128)(2,1)S(1)} async-done(((bf16[16,4,24,1024]{3,2,1,0:T(8,128)(2,1)}), bf16[16,4,24,1024]{3,2,1,0:T(8,128)(2,1)S(1)}, u32[]{:S(2)}, u32[]{:S(2)}) %all-to-all-start.1) | async-done | bytes 3145760 | tf_op jit(solution)/shard_map/all_to_all | solution.py:76
  323.7 5.3 %all-to-all-start.3 = ((bf16[16,4,24,1024]{3,2,1,0:T(8,128)(2,1)}), bf16[16,4,24,1024]{3,2,1,0:T(8,128)(2,1)}, u32[]{:S(2)}, u32[]{:S(2)}) async-start(bf16[16,4,24,1024]{3,2,1,0:T(8,128)(2,1)} %copy.50), calls=%async_computation.3 | async-start | bytes 6291456 | tf_op jit(solution)/shard_map/all_to_all | solution.py:87
  329.1 0.0 copy-done.4
  329.1 0.6 dynamic-slice
  330.3 5.4 %gather_fusion.1 = bf16[1024,1024]{1,0:T(8,128)(2,1)} fusion(bf16[1536,1024]{1,0:T(8,128)(2,1)S(1)} %bitcast.68, s32[1024]{0:T(1024)S(1)} %broadcast_clamp_fusion), kind=kCustom, calls=%fused_computation.1 | custom fusion | bytes 4198400 | tf_op jit(solution)/shard_map/gather | solution.py:88
  335.7 64.5 %all-to-all-done.3 = bf16[16,4,24,1024]{3,2,1,0:T(8,128)(2,1)} async-done(((bf16[16,4,24,1024]{3,2,1,0:T(8,128)(2,1)}), bf16[16,4,24,1024]{3,2,1,0:T(8,128)(2,1)}, u32[]{:S(2)}, u32[]{:S(2)}) %all-to-all-start.3) | async-done | bytes 3145760 | tf_op jit(solution)/shard_map/all_to_all | solution.py:87
  400.2 0.0 copy-start.1
  400.2 8.5 %gather_fusion.4 = bf16[1024,1024]{1,0:T(8,128)(2,1)} fusion(bf16[1536,1024]{1,0:T(8,128)(2,1)} %bitcast.16, s32[1024]{0:T(1024)S(1)} %broadcast_clamp_fusion), kind=kCustom, calls=%fused_computation.4 | custom fusion | bytes 4198400 | tf_op jit(solution)/shard_map/gather | solution.py:94
  408.7 0.0 copy-start.3
  408.7 3.9 bitcast_reduce_fusion
  412.5 0.0 copy-done.3
  412.5 2.1 fusion.6
  414.6 33.0 %all-reduce.3.cloned.1.call-done = bf16[1024,4,1152]{2,1,0:T(4,128)(2,1)} async-done(((bf16[1024,4,1152]{2,1,0:T(4,128)(2,1)}), bf16[1024,4,1152]{2,1,0:T(4,128)(2,1)}) %all-reduce.3.cloned.1.call-update) | async-done | bytes 9437200
  447.6 1.9 constant_dynamic-slice_fusion
  449.5 1.8 constant_dynamic-slice_fusion.1
  451.3 0.0 copy-done.1
  (9 shorter events, 0.1 us)
Async XLA Ops:
  7.2 228.9 %copy-start = (bf16[1024,4,384]{2,1,0:T(4,128)(2,1)S(1)}, bf16[1024,4,384]{2,1,0:T(4,128)(2,1)}, u32[]{:S(2)}) copy-start(bf16[1024,4,384]{2,1,0:T(4,128)(2,1)} %param.11) | copy-start | bytes 9437188
  48.6 10.4 %copy-start.2 = (bf16[128,1024]{1,0:T(8,128)(2,1)S(1)}, bf16[128,1024]{1,0:T(8,128)(2,1)}, u32[]{:S(2)}) copy-start(bf16[128,1024]{1,0:T(8,128)(2,1)} %param.9) | copy-start | bytes 786436
  161.9 74.2 %all-to-all-start.2 = ((bf16[16,4,24,1024]{3,2,1,0:T(8,128)(2,1)}), bf16[16,4,24,1024]{3,2,1,0:T(8,128)(2,1)}, u32[]{:S(2)}, u32[]{:S(2)}) async-start(bf16[16,4,24,1024]{3,2,1,0:T(8,128)(2,1)} %get-tuple-element.15), calls=%async_computation.2 | async-start | bytes 6291456 | tf_op jit(solution)/shard_map/all_to_all | solution.py:79
  243.4 1.9 copy-start.5
  247.3 76.5 %all-to-all-start.1 = ((bf16[16,4,24,1024]{3,2,1,0:T(8,128)(2,1)}), bf16[16,4,24,1024]{3,2,1,0:T(8,128)(2,1)S(1)}, u32[]{:S(2)}, u32[]{:S(2)}) async-start(bf16[16,4,24,1024]{3,2,1,0:T(8,128)(2,1)} %copy.44), calls=%async_computation.1 | async-start | bytes 6291456 | tf_op jit(solution)/shard_map/all_to_all | solution.py:76
  252.7 195.0 %all-reduce.3.cloned.1.call-start = ((), (), s32[]{:S(2)}) async-start(), calls=%async_computation.4 | async-start | bytes 18874368
  252.9 6.2 %copy-start.6 = (bf16[16,4,24,384]{3,2,0,1:T(8,128)(2,1)S(1)}, bf16[16,4,24,384]{3,2,0,1:T(8,128)(2,1)}, u32[]{:S(2)}) copy-start(bf16[16,4,24,384]{3,2,0,1:T(8,128)(2,1)} %copy-done.5) | copy-start | bytes 3538948
  294.6 34.5 %copy-start.4 = (u32[256]{0:T(256)S(1)}, u32[256]{0:T(256)}, u32[]{:S(2)}) copy-start(u32[256]{0:T(256)} %constant.49) | copy-start | bytes 3076
  323.7 76.4 %all-to-all-start.3 = ((bf16[16,4,24,1024]{3,2,1,0:T(8,128)(2,1)}), bf16[16,4,24,1024]{3,2,1,0:T(8,128)(2,1)}, u32[]{:S(2)}, u32[]{:S(2)}) async-start(bf16[16,4,24,1024]{3,2,1,0:T(8,128)(2,1)} %copy.50), calls=%async_computation.3 | async-start | bytes 6291456 | tf_op jit(solution)/shard_map/all_to_all | solution.py:87
  400.2 51.1 %copy-start.1 = (bf16[1024,4,384]{2,1,0:T(4,128)(2,1)S(1)}, bf16[1024,4,384]{2,1,0:T(4,128)(2,1)}, u32[]{:S(2)}) copy-start(bf16[1024,4,384]{2,1,0:T(4,128)(2,1)} %param.11) | copy-start | bytes 9437188
  408.7 3.9 copy-start.3
Sparse Core Ops, SparseCore 0:
  286.6 160.9 all-reduce.2
where the time goes:
time: 460 us; the launch traced here: 458 us
  waiting for transfers between devices  188 us (41%)
  blocking collectives  83.4 us (18%)
  local copies, waits for them, and re-layouts  71.1 us (15%)
  other arithmetic  51.8 us (11%)
  matrix products  33.8 us (7%)
  starting transfers between devices  15.5 us (3%)
  between operations  14.9 us (3%)
    all_to_all x1, blocking collectives, per_device(): lax.all_to_all(x_slots, 'expert', split_axis=0, concat_axis=0, tiled=True)  83.4 us
    all_to_all x1, waiting for transfers between devices, per_device(): lax.all_to_all(slot_grads, 'expert', split_axis=0, concat_axis=0, tiled=T...  64.5 us
    all_to_all x1, waiting for transfers between devices, per_device(): lax.all_to_all(cot_slots, 'expert', split_axis=0, concat_axis=0, tiled=True)  61 us
    unnamed x2, waiting for transfers between devices  33 us
    another operation x2, other arithmetic  31.1 us
    all_to_all x1, waiting for transfers between devices, per_device(): lax.all_to_all(expert_out, 'expert', split_axis=0, concat_axis=0, tiled=T...  29.1 us
    concatenate x1, local copies, waits for them, and re-layouts, per_device(): jnp.concatenate([term_gu, term_dn], axis=2).astype(jnp.bfloat16)  15.5 us
  transfers between devices with their start and end apart: 4, of which 4 were waited for; matrix products, arithmetic and copies ran while one was open for 15% of the time, Pallas kernels for 0%

commit v1 on v0

v1 whole, which is shorter than its diff:
```python
import jax
import jax.numpy as jnp
from jax import lax
from jax.experimental import pallas as pl
from jax.experimental.pallas import tpu as pltpu
from jax.sharding import PartitionSpec as P

MESH = pl.DeviceIdType.MESH
F32 = jnp.float32
BF16 = jnp.bfloat16

NZ = 8
NX = 4
TOK = 128
D = 1024
H = 384
F = 2 * H
W3 = 3 * H
L = 4
MOST = 24
PAIR = 2 * MOST
ROWS = L * PAIR
SLOTS = NZ * PAIR


def place(distance):
    return (distance + 2) % NZ


def dot(a, b, dims):
    return lax.dot_general(a, b, ((dims[:1], dims[1:]), ((), ())), preferred_element_type=F32)


def kernel(
    x_ref, rt_ref, gt_ref, c_ref, wgu_hbm, wdn_hbm,
    lo_ref, go_ref, ogu_ref, odn_ref,
    W, rawg, rawd, xg, cg, mg, Xs, Cs, GH, DP, Gs, Pm, OR, GR,
    sibo, sibg, rlp, rgp, rlm, rgm,
    fwd1, fin1, fwd2, fin2, fs,
    ring_s, ring_r, sib_s, sib_r, rsib_s, rsib_r, rz_s, rz_r, x1_s, x1_r, x2_s, x2_r, raw_sem,
):
    dp, ex = lax.axis_index("dp"), lax.axis_index("expert")
    yy, xx = dp // NX, dp % NX
    zz, core = ex // 2, ex % 2

    def at_z(step):
        return (dp, ((zz + step) % NZ) * 2 + core)

    def at_x(step):
        return (yy * NX + (xx + step) % NX, ex)

    def at_y(step):
        return (((yy + step) % NX) * NX + xx, ex)

    zp, zm, sib = at_z(1), at_z(NZ - 1), (dp, zz * 2 + 1 - core)
    xp, xm, yp, ym = at_x(1), at_x(NX - 1), at_y(1), at_y(NX - 1)

    def raw_copies(group):
        rows = pl.ds(group * 256, 256)
        return (
            pltpu.make_async_copy(wgu_hbm.at[rows], rawg, raw_sem.at[0]),
            pltpu.make_async_copy(wdn_hbm.at[rows], rawd, raw_sem.at[1]),
        )

    for copy in raw_copies(0):
        copy.start()

    mg[place(0), 0, 0:8, :] = rt_ref[...].astype(F32)
    mg[place(0), 0, 8:16, :] = gt_ref[...]

    barrier = pltpu.get_barrier_semaphore()
    for peer in (zp, zm, sib, xp, xm, yp, ym):
        pl.semaphore_signal(barrier, inc=1, device_id=peer, device_id_type=MESH)
    pl.semaphore_wait(barrier, 7)

    sends = []

    def send(src, dst, send_sem, recv_sem, peer):
        copy = pltpu.make_async_remote_copy(
            src_ref=src, dst_ref=dst, send_sem=send_sem, recv_sem=recv_sem,
            device_id=peer, device_id_type=MESH,
        )
        copy.start()
        sends.append(copy)

    def arrived(dst, recv_sem):
        pltpu.make_async_remote_copy(
            src_ref=dst, dst_ref=dst, send_sem=recv_sem, recv_sem=recv_sem,
            device_id=zp, device_id_type=MESH,
        ).wait_recv()

    def block(t, distance, column):
        if t == 2:
            return mg.at[place(distance), column]
        return (xg, cg)[t].at[place(distance), pl.ds(column * TOK, TOK)]

    far = {0: (4, 3), 1: (3, 4), 2: (4, 3)}
    own = {0: x_ref, 1: c_ref, 2: mg.at[place(0), 0]}
    for t in (2, 0, 1):
        send(own[t], block(t, NZ - 1, 0), ring_s.at[t, 0, 0], ring_r.at[t, NZ - 1], zp)
        send(own[t], block(t, 1, 0), ring_s.at[t, 1, 0], ring_r.at[t, 1], zm)
        send(own[t], block(t, 0, 1), sib_s.at[t, 0], sib_r.at[t, 0], sib)
    xg[place(0), 0:TOK] = x_ref[...]
    cg[place(0), 0:TOK] = c_ref[...]

    def hop(k, tensors):
        for t in tensors:
            for way, distance, peer, further in ((0, NZ - k, zp, NZ - k - 1), (1, k, zm, k + 1)):
                if k > far[t][way]:
                    continue
                arrived(block(t, distance, 0), ring_r.at[t, distance])
                if k < far[t][way]:
                    send(block(t, distance, 0), block(t, further, 0), ring_s.at[t, way, k], ring_r.at[t, further], peer)
                send(block(t, distance, 0), block(t, distance, 1), sib_s.at[t, distance], sib_r.at[t, distance], sib)

    def relayout(group):
        for copy in raw_copies(group):
            copy.wait()

        def body(i, carry):
            rows = pl.ds(i * 64, 64)
            W[:, group, i, :, 0:F] = jnp.swapaxes(rawg[rows], 0, 1)
            W[:, group, i, :, F:W3] = jnp.swapaxes(rawd[rows], 0, 1)
            return carry

        lax.fori_loop(0, NX, body, 0)
        if group < NX - 1:
            for copy in raw_copies(group + 1):
                copy.start()

    def dispatch(distance):
        for t in (2, 0, 1):
            arrived(block(t, distance, 1), sib_r.at[t, distance])
        i = place(distance)
        first = (ex * L).astype(F32)
        earlier = (
            lax.broadcasted_iota(jnp.int32, (TOK, TOK), 0) < lax.broadcasted_iota(jnp.int32, (TOK, TOK), 1)
        ).astype(BF16)
        slot = lax.broadcasted_iota(jnp.int32, (MOST, TOK), 0).astype(F32)
        sub = lax.broadcasted_iota(jnp.int32, (8, TOK), 0)
        empty = jnp.zeros((MOST, TOK), F32)
        pieces = [[None, None] for _ in range(L)]
        for c in range(2):
            named, gates = mg[i, c, 0:8, :], mg[i, c, 8:16, :]
            masks, weights = [], []
            stacked = jnp.zeros((8, TOK), F32)
            for l in range(L):
                hit = named == first + l
                mask = jnp.sum(hit.astype(F32), axis=0, keepdims=True)
                masks.append(mask)
                weights.append(jnp.sum(jnp.where(hit, gates, 0.0), axis=0, keepdims=True))
                stacked = jnp.where(sub == l, mask, stacked)
            rank = dot(stacked.astype(BF16), earlier, (1, 0))
            for l in range(L):
                chosen = jnp.where((slot == rank[l : l + 1]) & (masks[l] > 0.0), 1.0, 0.0)
                gate = jnp.sum(chosen * weights[l], axis=1, keepdims=True)
                Gs[l, i * PAIR + c * MOST : i * PAIR + (c + 1) * MOST, :] = jnp.broadcast_to(gate, (MOST, TOK))
                pieces[l][c] = jnp.concatenate([chosen, empty] if c == 0 else [empty, chosen], axis=1)
        picked = jnp.concatenate([pieces[l][c] for l in range(L) for c in range(2)], axis=0).astype(BF16)
        Pm[i] = picked
        for gathered, slots in ((xg, Xs), (cg, Cs)):
            got = dot(picked, gathered[i], (1, 0)).astype(BF16)
            for l in range(L):
                slots[l, i * PAIR : (i + 1) * PAIR, :] = got[l * PAIR : (l + 1) * PAIR]

    def experts(i0, i1):
        r0, r1 = i0 * PAIR, i1 * PAIR

        def body(l, carry):
            up_w = W[l, :, :, :, 0:F].reshape(D, F)
            down_w = W[l, :, :, :, F:W3].reshape(D, H)
            gate = Gs[l, r0:r1, 0:1]
            projected = dot(Xs[l, r0:r1], up_w, (1, 0))
            g, u = projected[:, :H], projected[:, H:]
            s = jax.nn.sigmoid(g)
            gs = g * s
            hidden = (gs * u * gate).astype(BF16)
            GH[l, r0:r1] = hidden
            d_hidden = dot(Cs[l, r0:r1], down_w, (1, 0)) * gate
            d_gate = d_hidden * u * s * (1.0 + g * (1.0 - s))
            d_proj = jnp.concatenate([d_gate, d_hidden * gs], axis=1).astype(BF16)
            DP[l, r0:r1] = d_proj
            out = dot(hidden, down_w, (1, 1)).astype(BF16)
            back = dot(d_proj, up_w, (1, 1)).astype(BF16)
            at = pl.ds(pl.multiple_of(l * PAIR, 16), PAIR)
            for i in range(i0, i1):
                part = slice((i - i0) * PAIR, (i - i0 + 1) * PAIR)
                OR[i, at, :] = out[part]
                GR[i, at, :] = back[part]
            return carry

        lax.fori_loop(0, L, body, 0)

    relayout(0)
    relayout(1)
    hop(1, (2, 0))
    relayout(2)
    dispatch(0)
    hop(1, (1,))
    relayout(3)
    dispatch(1)
    dispatch(NZ - 1)
    hop(2, (2, 0))
    hop(2, (1,))
    dispatch(2)
    dispatch(NZ - 2)
    hop(3, (2, 0))
    experts(0, 5)
    hop(3, (1,))
    dispatch(3)
    dispatch(NZ - 3)
    hop(4, (2, 0, 1))
    dispatch(4)
    experts(5, 8)
    for copy in sends:
        copy.wait_send()
    sends.clear()

    def gradients(l0, l1):
        def body(n, carry):
            l, q = l0 + n // NX, n % NX
            columns = pl.ds(pl.multiple_of(q * 256, 256), 256)
            W[l, q, :, :, 0:F] = dot(Xs[l, :, columns], DP[l], (0, 0)).astype(BF16).reshape(NX, 64, F)
            W[l, q, :, :, F:W3] = dot(Cs[l, :, columns], GH[l], (0, 0)).astype(BF16).reshape(NX, 64, H)
            return carry

        lax.fori_loop(0, (l1 - l0) * NX, body, 0)

    def piece1(h, l, q):
        return W.at[l, :, q] if h == 0 else W.at[l, q]

    def piece2(h, l, q):
        return W.at[l, q, xx] if h == 0 else W.at[l, yy, q]

    def axes(h, stage):
        along_x = (h == 0) == (stage == 1)
        return (xx, xp, xm) if along_x else (yy, yp, ym)

    def spread(stage, h):
        at, plus, minus = axes(h, stage)
        piece, fwd, fin, s, r = (
            (piece1, fwd1, fin1, x1_s, x1_r) if stage == 1 else (piece2, fwd2, fin2, x2_s, x2_r)
        )
        la, lb = 2 * h, 2 * h + 1
        send(piece(h, la, (at + 2) % NX), fwd.at[h, 0], s.at[h, 0, 0], r.at[h, 0, 0], plus)
        send(piece(h, lb, (at + 2) % NX), fwd.at[h, 1], s.at[h, 1, 0], r.at[h, 1, 0], minus)
        send(piece(h, lb, (at + 1) % NX), fin.at[h, 0, 1], s.at[h, 0, 1], r.at[h, 0, 1], plus)
        send(piece(h, la, (at + 3) % NX), fin.at[h, 1, 0], s.at[h, 1, 1], r.at[h, 1, 1], minus)

    def relay(stage, h):
        at, plus, minus = axes(h, stage)
        fwd, fin, s, r = (fwd1, fin1, x1_s, x1_r) if stage == 1 else (fwd2, fin2, x2_s, x2_r)
        for way, l, q, peer, slot in ((0, 2 * h, (at + 1) % NX, plus, 0), (1, 2 * h + 1, (at + 3) % NX, minus, 1)):
            arrived(fwd.at[h, way], r.at[h, way, 0])
            if stage == 1:

                def body(n, carry):
                    mine = W[l, n, q] if h == 0 else W[l, q, n]
                    fwd1[h, way, n] = (fwd1[h, way, n].astype(F32) + mine.astype(F32)).astype(BF16)
                    return carry

                lax.fori_loop(0, NX, body, 0)
            else:
                mine = W[l, q, xx] if h == 0 else W[l, yy, q]
                fwd2[h, way] = (fwd2[h, way].astype(F32) + mine.astype(F32)).astype(BF16)
            send(fwd.at[h, way], fin.at[h, way, slot], s.at[h, way, 2], r.at[h, way, 2], peer)

    def settle(stage, h):
        at, plus, minus = axes(h, stage)
        fin, r = (fin1, x1_r) if stage == 1 else (fin2, x2_r)
        for way, slot, n in ((0, 1, 1), (1, 0, 1), (0, 0, 2), (1, 1, 2)):
            arrived(fin.at[h, way, slot], r.at[h, way, n])
        for slot in range(2):
            l = 2 * h + slot
            if stage == 1:

                def body(n, carry):
                    a, b = (n, at) if h == 0 else (at, n)
                    total = W[l, a, b].astype(F32) + fin1[h, 0, slot, n].astype(F32) + fin1[h, 1, slot, n].astype(F32)
                    W[l, a, b] = total.astype(BF16)
                    return carry

                lax.fori_loop(0, NX, body, 0)
            else:
                total = W[l, yy, xx].astype(F32) + fin2[h, 0, slot].astype(F32) + fin2[h, 1, slot].astype(F32)
                fs[l] = total.astype(BF16)

    def combine(i0, i1):
        def body(i, carry):
            picked = Pm[i]
            xg[i] = dot(picked, OR[i], (0, 0)).astype(BF16)
            cg[i] = dot(picked, GR[i], (0, 0)).astype(BF16)
            return carry

        lax.fori_loop(i0, i1, body, 0)
        for i in range(i0, i1):
            send(xg.at[i, pl.ds(TOK, TOK)], sibo.at[i], rsib_s.at[0, i], rsib_r.at[0, i], sib)
            send(cg.at[i, pl.ds(TOK, TOK)], sibg.at[i], rsib_s.at[1, i], rsib_r.at[1, i], sib)

    def total_of(parts):
        total = parts[0].astype(F32)
        for part in parts[1:]:
            total = total + part.astype(F32)
        return total.astype(BF16)

    ways = (
        (0, 0, (4, 3, 2, 1), rlp, zp),
        (1, 1, (4, 5, 6, 7), rgm, zm),
        (1, 0, (3, 2, 1), rgp, zp),
        (0, 1, (5, 6, 7), rlm, zm),
    )

    def reduce_step(j):
        for t, way, targets, slots, peer in ways:
            if j >= len(targets):
                continue
            i = place(targets[j])
            mine, other = ((xg, sibo), (cg, sibg))[t]
            arrived(other.at[i], rsib_r.at[t, i])
            if j > 0:
                arrived(slots.at[j - 1], rz_r.at[t, way, j - 1])

            def body(n, carry):
                rows = pl.ds(pl.multiple_of(n * 32, 32), 32)
                parts = [mine[i, rows, :], other[i, rows, :]]
                if j > 0:
                    parts.append(slots[j - 1, rows, :])
                mine[i, rows, :] = total_of(parts)
                return carry

            lax.fori_loop(0, TOK // 32, body, 0)
            send(mine.at[i, pl.ds(0, TOK)], slots.at[j], rz_s.at[t, way, j], rz_r.at[t, way, j], peer)

    def reduce_end():
        i = place(0)
        for t, mine, other, plus, minus, out in ((0, xg, sibo, rlp, rlm, lo_ref), (1, cg, sibg, rgp, rgm, go_ref)):
            np_, nm = (3, 2) if t == 0 else (2, 3)
            arrived(other.at[i], rsib_r.at[t, i])
            arrived(plus.at[np_], rz_r.at[t, 0, np_])
            arrived(minus.at[nm], rz_r.at[t, 1, nm])

            def body(n, carry):
                rows = pl.ds(pl.multiple_of(n * 32, 32), 32)
                out[rows, :] = total_of([mine[i, rows, :], other[i, rows, :], plus[np_, rows, :], minus[nm, rows, :]])
                return carry

            lax.fori_loop(0, TOK // 32, body, 0)

    gradients(0, 2)
    spread(1, 0)
    combine(5, 8)
    gradients(2, 4)
    spread(1, 1)
    reduce_step(0)
    combine(0, 5)
    relay(1, 0)
    relay(1, 1)
    reduce_step(1)
    reduce_step(2)
    reduce_step(3)
    settle(1, 0)
    spread(2, 0)
    settle(1, 1)
    spread(2, 1)
    relay(2, 0)
    relay(2, 1)
    reduce_end()
    settle(2, 0)
    settle(2, 1)
    ogu_ref[...] = jnp.swapaxes(fs[:, :, 0:F], 0, 1)
    odn_ref[...] = jnp.swapaxes(fs[:, :, F:W3], 0, 1)
    for copy in sends:
        copy.wait_send()


def per_device(tokens, routes, gate_weights, cotangent, w_gate_up, w_down):
    vmem = pl.BlockSpec(memory_space=pltpu.VMEM)
    hbm = pl.BlockSpec(memory_space=pl.ANY)
    dma = pltpu.SemaphoreType.DMA
    rows = D // (NX * NX)
    return pl.pallas_call(
        kernel,
        out_shape=(
            jax.ShapeDtypeStruct((TOK, D), BF16),
            jax.ShapeDtypeStruct((TOK, D), BF16),
            jax.ShapeDtypeStruct((rows, L, F), BF16),
            jax.ShapeDtypeStruct((rows, L, H), BF16),
        ),
        in_specs=[vmem, vmem, vmem, vmem, hbm, hbm],
        out_specs=(vmem, vmem, vmem, vmem),
        scratch_shapes=[
            pltpu.VMEM((L, NX, NX, rows, W3), BF16),
            pltpu.VMEM((256, L, F), BF16),
            pltpu.VMEM((256, L, H), BF16),
            pltpu.VMEM((NZ, 2 * TOK, D), BF16),
            pltpu.VMEM((NZ, 2 * TOK, D), BF16),
            pltpu.VMEM((NZ, 2, 16, TOK), F32),
            pltpu.VMEM((L, SLOTS, D), BF16),
            pltpu.VMEM((L, SLOTS, D), BF16),
            pltpu.VMEM((L, SLOTS, H), BF16),
            pltpu.VMEM((L, SLOTS, F), BF16),
            pltpu.VMEM((L, SLOTS, TOK), F32),
            pltpu.VMEM((NZ, ROWS, 2 * TOK), BF16),
            pltpu.VMEM((NZ, ROWS, D), BF16),
            pltpu.VMEM((NZ, ROWS, D), BF16),
            pltpu.VMEM((NZ, TOK, D), BF16),
            pltpu.VMEM((NZ, TOK, D), BF16),
            pltpu.VMEM((4, TOK, D), BF16),
            pltpu.VMEM((3, TOK, D), BF16),
            pltpu.VMEM((3, TOK, D), BF16),
            pltpu.VMEM((4, TOK, D), BF16),
            pltpu.VMEM((2, 2, NX, rows, W3), BF16),
            pltpu.VMEM((2, 2, 2, NX, rows, W3), BF16),
            pltpu.VMEM((2, 2, rows, W3), BF16),
            pltpu.VMEM((2, 2, 2, rows, W3), BF16),
            pltpu.VMEM((L, rows, W3), BF16),
            dma((3, 2, 4)), dma((3, NZ)), dma((3, NZ)), dma((3, NZ)),
            dma((2, NZ)), dma((2, NZ)), dma((2, 2, 4)), dma((2, 2, 4)),
            dma((2, 2, 3)), dma((2, 2, 3)), dma((2, 2, 3)), dma((2, 2, 3)),
            dma((2,)),
        ],
        compiler_params=pltpu.CompilerParams(
            collective_id=0, has_side_effects=True, vmem_limit_bytes=63 << 20
        ),
    )(tokens, routes.T, gate_weights.T, cotangent, w_gate_up, w_down)


def solution(mesh):
    rows = P(("dp", "expert"), None)
    return jax.shard_map(
        per_device,
        mesh=mesh,
        in_specs=(rows, rows, rows, rows, P(None, "expert", None), P(None, "expert", None)),
        out_specs=(rows, rows, P("dp", "expert", None), P("dp", "expert", None)),
        check_vma=False,
    )
```

time: 460 us -> 134 us (0.29)
  waiting for transfers between devices: 188 us -> 0 us
  Pallas kernels: 0 us -> 126 us
  blocking collectives: 83.4 us -> 0 us
  local copies, waits for them, and re-layouts: 71.1 us -> 6.89 us
  other arithmetic: 51.8 us -> 0 us
  matrix products: 33.8 us -> 0 us
  starting transfers between devices: 15.5 us -> 0 us
  between operations: 14.9 us -> 0.64 us
    all_to_all x3 -> x0, waiting for transfers between devices: 155 us -> none  [the longest x1 64.5 us: per_device(): lax.all_to_all(slot_grads, 'expert', split_axis=0, concat_axis=0, tiled=T...]
    pallas_call x0 -> x1, Pallas kernels: none -> 126 us  [per_device(): pl.pallas_call(kernel, out_shape=(jax.ShapeDtypeStruct((TOK, D), BF16), j...]
    all_to_all x1 -> x0, blocking collectives: 83.4 us -> none  [per_device(): lax.all_to_all(x_slots, 'expert', split_axis=0, concat_axis=0, tiled=True)]
    gather x5 -> x0, local copies, waits for them, and re-layouts: 34.3 us -> none  [the longest x1 8.77 us: per_device(): tokens[token_of]]
    dot_general x6 -> x0, matrix products: 33.8 us -> none  [the longest x1 8.58 us: forward_local(): jnp.einsum('slmd,dlf->slmf', received, w_gate_up, preferred_element_type=...]
    unnamed x2 -> x0, waiting for transfers between devices: 33 us -> none
    another operation x2 -> x0, other arithmetic: 31.1 us -> none
    concatenate x1 -> x0, local copies, waits for them, and re-layouts: 15.5 us -> none  [per_device(): jnp.concatenate([term_gu, term_dn], axis=2).astype(jnp.bfloat16)]
  transfers between devices with their start and end apart: 4 -> 0, of which waited for: 4 -> 0; matrix products, arithmetic and copies ran while one was open for 15% -> 0% of each run, Pallas kernels for 0% -> 0%
where the time goes in v1:
time: 134 us; the launch traced here: 133 us
  Pallas kernels  126 us (94%)
  local copies, waits for them, and re-layouts  6.89 us (5%)
    pallas_call x1, Pallas kernels, per_device(): pl.pallas_call(kernel, out_shape=(jax.ShapeDtypeStruct((TOK, D), BF16), j...  126 us
    unnamed x4, local copies, waits for them, and re-layouts  6.89 us

profile of v1, /device:TPU:1, one launch (start us, length us, event | category | flops | bytes accessed | tf_op | source)
XLA Modules:
  0.0 133.3 jit_solution(680321567941304725)
XLA Ops:
  0.6 125.8 %shard_map.93 = (bf16[128,1024]{1,0:T(8,128)(2,1)}, bf16[128,1024]{1,0:T(8,128)(2,1)}, bf16[64,4,768]{2,1,0:T(4,128)(2,1)}, bf16[64,4,384]{2,1,0:T(4,128)(2,1)}) custom-call(bf16[128,1024]{1,0:T(8,128)(2,1)} %x_ref.1, s32[8,128]{1,0:T(8,128)} %bitcast.2, f32[8,128]{1,0:T(8,128)} %bitcast.3, bf16[128,1024]{1,0:T(8,128)(2,1)} %c_ref.1, ...), custom_call_target="tpu_custom_call" | custom-call | tf_op jit(solution)/shard_map/pallas_call | solution.py:381
  126.4 1.7 %copy.14 = bf16[128,1024]{1,0:T(8,128)(2,1)} copy(bf16[128,1024]{1,0:T(8,128)(2,1)} %get-tuple-element.8) | data formatting | bytes 524288
  128.1 1.7 %copy.15 = bf16[128,1024]{1,0:T(8,128)(2,1)} copy(bf16[128,1024]{1,0:T(8,128)(2,1)} %get-tuple-element.9) | data formatting | bytes 524288
  129.8 1.9 %copy.16 = bf16[64,4,768]{2,1,0:T(4,128)(2,1)} copy(bf16[64,4,768]{2,1,0:T(4,128)(2,1)} %get-tuple-element.10) | data formatting | bytes 786432
  131.6 1.7 %copy.17 = bf16[64,4,384]{2,1,0:T(4,128)(2,1)} copy(bf16[64,4,384]{2,1,0:T(4,128)(2,1)} %get-tuple-element.11) | data formatting | bytes 393216

commit v2 on v1

--- a/solution.py
+++ b/solution.py
@@ -23,8 +23,11 @@
 SLOTS = NZ * PAIR
 
 
+ORDER = (0, 1, 7, 2, 6, 3, 5, 4)
+
+
 def place(distance):
-    return (distance + 2) % NZ
+    return ORDER.index(distance)
 
 
 def dot(a, b, dims):
@@ -32,12 +35,12 @@
 
 
 def kernel(
-    x_ref, rt_ref, gt_ref, c_ref, wgu_hbm, wdn_hbm,
+    x_hbm, rt_ref, gt_ref, c_hbm, wgu_hbm, wdn_hbm,
     lo_ref, go_ref, ogu_ref, odn_ref,
     W, rawg, rawd, xg, cg, mg, Xs, Cs, GH, DP, Gs, Pm, OR, GR,
     sibo, sibg, rlp, rgp, rlm, rgm,
     fwd1, fin1, fwd2, fin2, fs,
-    ring_s, ring_r, sib_s, sib_r, rsib_s, rsib_r, rz_s, rz_r, x1_s, x1_r, x2_s, x2_r, raw_sem,
+    ring_s, ring_r, sib_s, sib_r, rsib_s, rsib_r, rz_s, rz_r, x1_s, x1_r, x2_s, x2_r, raw_sem, own_sem,
 ):
     dp, ex = lax.axis_index("dp"), lax.axis_index("expert")
     yy, xx = dp // NX, dp % NX
@@ -62,7 +65,11 @@
             pltpu.make_async_copy(wdn_hbm.at[rows], rawd, raw_sem.at[1]),
         )
 
-    for copy in raw_copies(0):
+    own_copies = [
+        pltpu.make_async_copy(source, gathered.at[place(0), pl.ds(0, TOK)], own_sem.at[n])
+        for n, (source, gathered) in enumerate(((x_hbm, xg), (c_hbm, cg)))
+    ]
+    for copy in own_copies + list(raw_copies(0)):
         copy.start()
 
     mg[place(0), 0, 0:8, :] = rt_ref[...].astype(F32)
@@ -73,15 +80,15 @@
         pl.semaphore_signal(barrier, inc=1, device_id=peer, device_id_type=MESH)
     pl.semaphore_wait(barrier, 7)
 
-    sends = []
-
-    def send(src, dst, send_sem, recv_sem, peer):
+    sends, reading = [], {}
+
+    def send(src, dst, send_sem, recv_sem, peer, source_place=None):
         copy = pltpu.make_async_remote_copy(
             src_ref=src, dst_ref=dst, send_sem=send_sem, recv_sem=recv_sem,
             device_id=peer, device_id_type=MESH,
         )
         copy.start()
-        sends.append(copy)
+        (sends if source_place is None else reading.setdefault(source_place, [])).append(copy)
 
     def arrived(dst, recv_sem):
         pltpu.make_async_remote_copy(
@@ -95,13 +102,11 @@
         return (xg, cg)[t].at[place(distance), pl.ds(column * TOK, TOK)]
 
     far = {0: (4, 3), 1: (3, 4), 2: (4, 3)}
-    own = {0: x_ref, 1: c_ref, 2: mg.at[place(0), 0]}
+    own = {0: x_hbm, 1: c_hbm, 2: mg.at[place(0), 0]}
     for t in (2, 0, 1):
         send(own[t], block(t, NZ - 1, 0), ring_s.at[t, 0, 0], ring_r.at[t, NZ - 1], zp)
         send(own[t], block(t, 1, 0), ring_s.at[t, 1, 0], ring_r.at[t, 1], zm)
         send(own[t], block(t, 0, 1), sib_s.at[t, 0], sib_r.at[t, 0], sib)
-    xg[place(0), 0:TOK] = x_ref[...]
-    cg[place(0), 0:TOK] = c_ref[...]
 
     def hop(k, tensors):
         for t in tensors:
@@ -110,8 +115,8 @@
                     continue
                 arrived(block(t, distance, 0), ring_r.at[t, distance])
                 if k < far[t][way]:
-                    send(block(t, distance, 0), block(t, further, 0), ring_s.at[t, way, k], ring_r.at[t, further], peer)
-                send(block(t, distance, 0), block(t, distance, 1), sib_s.at[t, distance], sib_r.at[t, distance], sib)
+                    send(block(t, distance, 0), block(t, further, 0), ring_s.at[t, way, k], ring_r.at[t, further], peer, place(distance))
+                send(block(t, distance, 0), block(t, distance, 1), sib_s.at[t, distance], sib_r.at[t, distance], sib, place(distance))
 
     def relayout(group):
         for copy in raw_copies(group):
@@ -191,100 +196,6 @@
 
         lax.fori_loop(0, L, body, 0)
 
-    relayout(0)
-    relayout(1)
-    hop(1, (2, 0))
-    relayout(2)
-    dispatch(0)
-    hop(1, (1,))
-    relayout(3)
-    dispatch(1)
-    dispatch(NZ - 1)
-    hop(2, (2, 0))
-    hop(2, (1,))
-    dispatch(2)
-    dispatch(NZ - 2)
-    hop(3, (2, 0))
-    experts(0, 5)
-    hop(3, (1,))
-    dispatch(3)
-    dispatch(NZ - 3)
-    hop(4, (2, 0, 1))
-    dispatch(4)
-    experts(5, 8)
-    for copy in sends:
-        copy.wait_send()
-    sends.clear()
-
-    def gradients(l0, l1):
-        def body(n, carry):
-            l, q = l0 + n // NX, n % NX
-            columns = pl.ds(pl.multiple_of(q * 256, 256), 256)
-            W[l, q, :, :, 0:F] = dot(Xs[l, :, columns], DP[l], (0, 0)).astype(BF16).reshape(NX, 64, F)
-            W[l, q, :, :, F:W3] = dot(Cs[l, :, columns], GH[l], (0, 0)).astype(BF16).reshape(NX, 64, H)
-            return carry
-
-        lax.fori_loop(0, (l1 - l0) * NX, body, 0)
-
-    def piece1(h, l, q):
-        return W.at[l, :, q] if h == 0 else W.at[l, q]
-
-    def piece2(h, l, q):
-        return W.at[l, q, xx] if h == 0 else W.at[l, yy, q]
-
-    def axes(h, stage):
-        along_x = (h == 0) == (stage == 1)
-        return (xx, xp, xm) if along_x else (yy, yp, ym)
-
-    def spread(stage, h):
-        at, plus, minus = axes(h, stage)
-        piece, fwd, fin, s, r = (
-            (piece1, fwd1, fin1, x1_s, x1_r) if stage == 1 else (piece2, fwd2, fin2, x2_s, x2_r)
-        )
-        la, lb = 2 * h, 2 * h + 1
-        send(piece(h, la, (at + 2) % NX), fwd.at[h, 0], s.at[h, 0, 0], r.at[h, 0, 0], plus)
-        send(piece(h, lb, (at + 2) % NX), fwd.at[h, 1], s.at[h, 1, 0], r.at[h, 1, 0], minus)
-        send(piece(h, lb, (at + 1) % NX), fin.at[h, 0, 1], s.at[h, 0, 1], r.at[h, 0, 1], plus)
-        send(piece(h, la, (at + 3) % NX), fin.at[h, 1, 0], s.at[h, 1, 1], r.at[h, 1, 1], minus)
-
-    def relay(stage, h):
-        at, plus, minus = axes(h, stage)
-        fwd, fin, s, r = (fwd1, fin1, x1_s, x1_r) if stage == 1 else (fwd2, fin2, x2_s, x2_r)
-        for way, l, q, peer, slot in ((0, 2 * h, (at + 1) % NX, plus, 0), (1, 2 * h + 1, (at + 3) % NX, minus, 1)):
-            arrived(fwd.at[h, way], r.at[h, way, 0])
-            if stage == 1:
-
-                def body(n, carry):
-                    mine = W[l, n, q] if h == 0 else W[l, q, n]
-                    fwd1[h, way, n] = (fwd1[h, way, n].astype(F32) + mine.astype(F32)).astype(BF16)
-                    return carry
-
-                lax.fori_loop(0, NX, body, 0)
-            else:
-                mine = W[l, q, xx] if h == 0 else W[l, yy, q]
-                fwd2[h, way] = (fwd2[h, way].astype(F32) + mine.astype(F32)).astype(BF16)
-            send(fwd.at[h, way], fin.at[h, way, slot], s.at[h, way, 2], r.at[h, way, 2], peer)
-
-    def settle(stage, h):
-        at, plus, minus = axes(h, stage)
-        fin, r = (fin1, x1_r) if stage == 1 else (fin2, x2_r)
-        for way, slot, n in ((0, 1, 1), (1, 0, 1), (0, 0, 2), (1, 1, 2)):
-            arrived(fin.at[h, way, slot], r.at[h, way, n])
-        for slot in range(2):
-            l = 2 * h + slot
-            if stage == 1:
-
-                def body(n, carry):
-                    a, b = (n, at) if h == 0 else (at, n)
-                    total = W[l, a, b].astype(F32) + fin1[h, 0, slot, n].astype(F32) + fin1[h, 1, slot, n].astype(F32)
-                    W[l, a, b] = total.astype(BF16)
-                    return carry
-
-                lax.fori_loop(0, NX, body, 0)
-            else:
-                total = W[l, yy, xx].astype(F32) + fin2[h, 0, slot].astype(F32) + fin2[h, 1, slot].astype(F32)
-                fs[l] = total.astype(BF16)
-
     def combine(i0, i1):
         def body(i, carry):
             picked = Pm[i]
@@ -292,10 +203,121 @@
             cg[i] = dot(picked, GR[i], (0, 0)).astype(BF16)
             return carry
 
+        for i in range(i0, i1):
+            for copy in reading.pop(i, []):
+                copy.wait_send()
         lax.fori_loop(i0, i1, body, 0)
         for i in range(i0, i1):
             send(xg.at[i, pl.ds(TOK, TOK)], sibo.at[i], rsib_s.at[0, i], rsib_r.at[0, i], sib)
             send(cg.at[i, pl.ds(TOK, TOK)], sibg.at[i], rsib_s.at[1, i], rsib_r.at[1, i], sib)
+
+    for group in range(NX):
+        relayout(group)
+    for copy in own_copies:
+        copy.wait()
+    hop(1, (2, 0))
+    hop(1, (1,))
+    for distance in (0, 1, 7):
+        dispatch(distance)
+    experts(0, 3)
+    hop(2, (2, 0))
+    hop(2, (1,))
+    dispatch(2)
+    dispatch(6)
+    experts(3, 5)
+    combine(0, 3)
+    hop(3, (2, 0))
+    hop(3, (1,))
+    dispatch(3)
+    dispatch(5)
+    experts(5, 7)
+    combine(3, 5)
+    hop(4, (2, 0, 1))
+    dispatch(4)
+    experts(7, 8)
+
+    def gradient(l, q):
+        columns = pl.ds(pl.multiple_of(q * 256, 256), 256)
+        W[l, q, :, :, 0:F] = dot(Xs[l, :, columns], DP[l], (0, 0)).astype(BF16).reshape(NX, 64, F)
+        W[l, q, :, :, F:W3] = dot(Cs[l, :, columns], GH[l], (0, 0)).astype(BF16).reshape(NX, 64, H)
+
+    def chunk(h, l, q, n):
+        return (l, n, q) if h == 0 else (l, q, n)
+
+    def axes(h, stage):
+        along_x = (h == 0) == (stage == 1)
+        return (xx, xp, xm) if along_x else (yy, yp, ym)
+
+    def second(h, o):
+        return (axes(h, 2)[0] + o) % NX
+
+    def far1(h, way, o):
+        at, plus, minus = axes(h, 1)
+        n = second(h, o)
+        send(
+            W.at[chunk(h, 2 * h + way, (at + 2) % NX, n)], fwd1.at[h, way, n],
+            x1_s.at[h, way, o], x1_r.at[h, way, o], (plus, minus)[way],
+        )
+
+    def near1(h, way):
+        at, plus, minus = axes(h, 1)
+        l, q = 2 * h + 1 - way, (at + (1, 3)[way]) % NX
+        source = W.at[l, :, q] if h == 0 else W.at[l, q]
+        send(source, fin1.at[h, way, 1 - way], x1_s.at[h, way, 4], x1_r.at[h, way, 4], (plus, minus)[way])
+
+    def relay1(h, way, o):
+        at, plus, minus = axes(h, 1)
+        n = second(h, o)
+        arrived(fwd1.at[h, way, n], x1_r.at[h, way, o])
+        mine = W[chunk(h, 2 * h + way, (at + (1, 3)[way]) % NX, n)]
+        fwd1[h, way, n] = (fwd1[h, way, n].astype(F32) + mine.astype(F32)).astype(BF16)
+        send(
+            fwd1.at[h, way, n], fin1.at[h, way, way, n],
+            x1_s.at[h, way, 5 + o], x1_r.at[h, way, 5 + o], (plus, minus)[way],
+        )
+
+    def settle1(h, o):
+        at = axes(h, 1)[0]
+        n = second(h, o)
+        for way in range(2):
+            if o == 2:
+                arrived(fin1.at[h, way, 1 - way], x1_r.at[h, way, 4])
+            arrived(fin1.at[h, way, way, n], x1_r.at[h, way, 5 + o])
+        for slot in range(2):
+            own = chunk(h, 2 * h + slot, at, n)
+            total = W[own].astype(F32) + fin1[h, 0, slot, n].astype(F32) + fin1[h, 1, slot, n].astype(F32)
+            W[own] = total.astype(BF16)
+
+    def held(h, l, q):
+        return chunk(h, l, axes(h, 1)[0], q)
+
+    def far2(h):
+        for way in range(2):
+            send(
+                W.at[held(h, 2 * h + way, second(h, 2))], fwd2.at[h, way],
+                x2_s.at[h, way, 0], x2_r.at[h, way, 0], axes(h, 2)[1 + way],
+            )
+
+    def near2(h, way):
+        send(
+            W.at[held(h, 2 * h + 1 - way, second(h, (1, 3)[way]))], fin2.at[h, way, 1 - way],
+            x2_s.at[h, way, 1], x2_r.at[h, way, 1], axes(h, 2)[1 + way],
+        )
+
+    def relay2(h, way):
+        arrived(fwd2.at[h, way], x2_r.at[h, way, 0])
+        mine = W[held(h, 2 * h + way, second(h, (1, 3)[way]))]
+        fwd2[h, way] = (fwd2[h, way].astype(F32) + mine.astype(F32)).astype(BF16)
+        send(fwd2.at[h, way], fin2.at[h, way, way], x2_s.at[h, way, 2], x2_r.at[h, way, 2], axes(h, 2)[1 + way])
+
+    def settle2(h):
+        for way in range(2):
+            arrived(fin2.at[h, way, 1 - way], x2_r.at[h, way, 1])
+            arrived(fin2.at[h, way, way], x2_r.at[h, way, 2])
+        for slot in range(2):
+            l = 2 * h + slot
+            total = W[l, yy, xx].astype(F32) + fin2[h, 0, slot].astype(F32) + fin2[h, 1, slot].astype(F32)
+            fs[l] = total.astype(BF16)
 
     def total_of(parts):
         total = parts[0].astype(F32)
@@ -310,67 +332,100 @@
         (0, 1, (5, 6, 7), rlm, zm),
     )
 
+    HALF = TOK // 2
+
     def reduce_step(j):
-        for t, way, targets, slots, peer in ways:
-            if j >= len(targets):
-                continue
-            i = place(targets[j])
-            mine, other = ((xg, sibo), (cg, sibg))[t]
-            arrived(other.at[i], rsib_r.at[t, i])
-            if j > 0:
-                arrived(slots.at[j - 1], rz_r.at[t, way, j - 1])
-
-            def body(n, carry):
-                rows = pl.ds(pl.multiple_of(n * 32, 32), 32)
+        for part in range(2):
+            rows = slice(part * HALF, (part + 1) * HALF)
+            span = pl.ds(part * HALF, HALF)
+            for t, way, targets, slots, peer in ways:
+                if j >= len(targets):
+                    continue
+                i = place(targets[j])
+                mine, other = ((xg, sibo), (cg, sibg))[t]
+                if part == 0:
+                    arrived(other.at[i], rsib_r.at[t, i])
                 parts = [mine[i, rows, :], other[i, rows, :]]
                 if j > 0:
+                    arrived(slots.at[j - 1, span], rz_r.at[t, way, j - 1, part])
                     parts.append(slots[j - 1, rows, :])
                 mine[i, rows, :] = total_of(parts)
-                return carry
-
-            lax.fori_loop(0, TOK // 32, body, 0)
-            send(mine.at[i, pl.ds(0, TOK)], slots.at[j], rz_s.at[t, way, j], rz_r.at[t, way, j], peer)
+                send(mine.at[i, span], slots.at[j, span], rz_s.at[t, way, j, part], rz_r.at[t, way, j, part], peer)
 
     def reduce_end():
         i = place(0)
-        for t, mine, other, plus, minus, out in ((0, xg, sibo, rlp, rlm, lo_ref), (1, cg, sibg, rgp, rgm, go_ref)):
-            np_, nm = (3, 2) if t == 0 else (2, 3)
-            arrived(other.at[i], rsib_r.at[t, i])
-            arrived(plus.at[np_], rz_r.at[t, 0, np_])
-            arrived(minus.at[nm], rz_r.at[t, 1, nm])
-
-            def body(n, carry):
-                rows = pl.ds(pl.multiple_of(n * 32, 32), 32)
+        for part in range(2):
+            rows = slice(part * HALF, (part + 1) * HALF)
+            span = pl.ds(part * HALF, HALF)
+            for t, mine, other, plus, minus, out in ((0, xg, sibo, rlp, rlm, lo_ref), (1, cg, sibg, rgp, rgm, go_ref)):
+                np_, nm = (3, 2) if t == 0 else (2, 3)
+                if part == 0:
+                    arrived(other.at[i], rsib_r.at[t, i])
+                arrived(plus.at[np_, span], rz_r.at[t, 0, np_, part])
+                arrived(minus.at[nm, span], rz_r.at[t, 1, nm, part])
                 out[rows, :] = total_of([mine[i, rows, :], other[i, rows, :], plus[np_, rows, :], minus[nm, rows, :]])
-                return carry
-
-            lax.fori_loop(0, TOK // 32, body, 0)
-
-    gradients(0, 2)
-    spread(1, 0)
-    combine(5, 8)
-    gradients(2, 4)
-    spread(1, 1)
+
+    def gradients(h, way, o):
+        gradient(2 * h + way, (yy + o) % NX)
+
+    for way in range(2):
+        gradients(0, way, 2)
+        far1(0, way, 2)
+    for way in range(2):
+        gradients(1, way, 2)
+        for o in (2, 1, 3, 0):
+            far1(1, way, o)
+    combine(7, 8)
+    combine(5, 7)
+    for way in range(2):
+        gradients(0, way, 1)
+        far1(0, way, 1)
     reduce_step(0)
-    combine(0, 5)
-    relay(1, 0)
-    relay(1, 1)
+    for o in (3, 0):
+        for way in range(2):
+            gradients(0, way, o)
+            far1(0, way, o)
+    near1(0, 0)
+    near1(0, 1)
+    gradients(1, 1, 1)
+    near1(1, 0)
+    gradients(1, 0, 3)
+    near1(1, 1)
+    gradients(1, 0, 1)
+    gradients(1, 1, 3)
+    gradients(1, 0, 0)
+    gradients(1, 1, 0)
     reduce_step(1)
+    for o in (2, 1, 3, 0):
+        for h in range(2):
+            for way in range(2):
+                relay1(h, way, o)
     reduce_step(2)
+    for h in range(2):
+        settle1(h, 2)
+        far2(h)
     reduce_step(3)
-    settle(1, 0)
-    spread(2, 0)
-    settle(1, 1)
-    spread(2, 1)
-    relay(2, 0)
-    relay(2, 1)
+    for o, way in ((1, 0), (3, 1)):
+        for h in range(2):
+            settle1(h, o)
+            near2(h, way)
+    for h in range(2):
+        for way in range(2):
+            relay2(h, way)
+    settle1(0, 0)
+    settle1(1, 0)
     reduce_end()
-    settle(2, 0)
-    settle(2, 1)
+    settle2(0)
+    settle2(1)
     ogu_ref[...] = jnp.swapaxes(fs[:, :, 0:F], 0, 1)
     odn_ref[...] = jnp.swapaxes(fs[:, :, F:W3], 0, 1)
     for copy in sends:
         copy.wait_send()
+
+
+def move(*refs):
+    for n in range(4):
+        refs[4 + n][...] = refs[n][...]
 
 
 def per_device(tokens, routes, gate_weights, cotangent, w_gate_up, w_down):
@@ -378,7 +433,7 @@
     hbm = pl.BlockSpec(memory_space=pl.ANY)
     dma = pltpu.SemaphoreType.DMA
     rows = D // (NX * NX)
-    return pl.pallas_call(
+    results = pl.pallas_call(
         kernel,
         out_shape=(
             jax.ShapeDtypeStruct((TOK, D), BF16),
@@ -386,7 +441,7 @@
             jax.ShapeDtypeStruct((rows, L, F), BF16),
             jax.ShapeDtypeStruct((rows, L, H), BF16),
         ),
-        in_specs=[vmem, vmem, vmem, vmem, hbm, hbm],
+        in_specs=[hbm, vmem, vmem, hbm, hbm, hbm],
         out_specs=(vmem, vmem, vmem, vmem),
         scratch_shapes=[
             pltpu.VMEM((L, NX, NX, rows, W3), BF16),
@@ -415,14 +470,20 @@
             pltpu.VMEM((2, 2, 2, rows, W3), BF16),
             pltpu.VMEM((L, rows, W3), BF16),
             dma((3, 2, 4)), dma((3, NZ)), dma((3, NZ)), dma((3, NZ)),
-            dma((2, NZ)), dma((2, NZ)), dma((2, 2, 4)), dma((2, 2, 4)),
-            dma((2, 2, 3)), dma((2, 2, 3)), dma((2, 2, 3)), dma((2, 2, 3)),
-            dma((2,)),
+            dma((2, NZ)), dma((2, NZ)), dma((2, 2, 4, 2)), dma((2, 2, 4, 2)),
+            dma((2, 2, 9)), dma((2, 2, 9)), dma((2, 2, 3)), dma((2, 2, 3)),
+            dma((2,)), dma((2,)),
         ],
         compiler_params=pltpu.CompilerParams(
             collective_id=0, has_side_effects=True, vmem_limit_bytes=63 << 20
         ),
     )(tokens, routes.T, gate_weights.T, cotangent, w_gate_up, w_down)
+    return pl.pallas_call(
+        move,
+        out_shape=tuple(jax.ShapeDtypeStruct(a.shape, a.dtype) for a in results),
+        in_specs=[vmem] * 4,
+        out_specs=(vmem,) * 4,
+    )(*results)
 
 
 def solution(mesh):

time: 134 us -> 123 us (0.918)
  local copies, waits for them, and re-layouts: 6.89 us -> 0 us
  Pallas kernels: 126 us -> 122 us
    unnamed x4 -> x0, local copies, waits for them, and re-layouts: 6.89 us -> none
    pallas_call x1, Pallas kernels: 126 us -> 120 us  [per_device(): pl.pallas_call(kernel, out_shape=(jax.ShapeDtypeStruct((TOK, D), BF16), j...]
    pallas_call x0 -> x1, Pallas kernels: none -> 2.2 us  [per_device(): pl.pallas_call(move, out_shape=tuple((jax.ShapeDtypeStruct(a.shape, a.dty...]
where the time goes in v2:
time: 123 us
  Pallas kernels  122 us (99%)
    pallas_call x1, Pallas kernels, per_device(): pl.pallas_call(kernel, out_shape=(jax.ShapeDtypeStruct((TOK, D), BF16), j...  120 us

profile of v2, /device:TPU:1, one launch (start us, length us, event | category | flops | bytes accessed | tf_op | source)
XLA Modules:
  0.0 123.0 jit_solution(8418190473993954087)
XLA Ops:
  0.6 120.1 %shard_map.93 = (bf16[128,1024]{1,0:T(8,128)(2,1)}, bf16[128,1024]{1,0:T(8,128)(2,1)}, bf16[64,4,768]{2,1,0:T(4,128)(2,1)}, bf16[64,4,384]{2,1,0:T(4,128)(2,1)}) custom-call(bf16[128,1024]{1,0:T(8,128)(2,1)} %x_hbm.1, s32[8,128]{1,0:T(8,128)} %bitcast.2, f32[8,128]{1,0:T(8,128)} %bitcast.3, bf16[128,1024]{1,0:T(8,128)(2,1)} %c_hbm.1, ...), custom_call_target="tpu_custom_call" | custom-call | tf_op jit(solution)/shard_map/pallas_call | solution.py:436
  120.7 2.2 %shard_map.94 = (bf16[128,1024]{1,0:T(8,128)(2,1)}, bf16[128,1024]{1,0:T(8,128)(2,1)}, bf16[64,4,768]{2,1,0:T(4,128)(2,1)}, bf16[64,4,384]{2,1,0:T(4,128)(2,1)}) custom-call(bf16[128,1024]{1,0:T(8,128)(2,1)} %get-tuple-element.8.refs_0_, bf16[128,1024]{1,0:T(8,128)(2,1)} %get-tuple-element.9.refs_1_, bf16[64,4,768]{2,1,0:T(4,128)(2,1)} %get-tuple-element.10.refs_2_, ...), custom_call_target="tpu_custom_call" | custom-call | tf_op jit(solution)/shard_map/pallas_call | solution.py:481

commit v3 on v2

--- a/solution.py
+++ b/solution.py
@@ -37,7 +37,7 @@
 def kernel(
     x_hbm, rt_ref, gt_ref, c_hbm, wgu_hbm, wdn_hbm,
     lo_ref, go_ref, ogu_ref, odn_ref,
-    W, rawg, rawd, xg, cg, mg, Xs, Cs, GH, DP, Gs, Pm, OR, GR,
+    W, Q, rawg, rawd, xg, cg, mg, Xs, Cs, GH, DP, Gs, Pm, OR, GR,
     sibo, sibg, rlp, rgp, rlm, rgm,
     fwd1, fin1, fwd2, fin2, fs,
     ring_s, ring_r, sib_s, sib_r, rsib_s, rsib_r, rz_s, rz_r, x1_s, x1_r, x2_s, x2_r, raw_sem, own_sem,
@@ -102,11 +102,11 @@
         return (xg, cg)[t].at[place(distance), pl.ds(column * TOK, TOK)]
 
     far = {0: (4, 3), 1: (3, 4), 2: (4, 3)}
-    own = {0: x_hbm, 1: c_hbm, 2: mg.at[place(0), 0]}
+    mine_of = {0: x_hbm, 1: c_hbm, 2: mg.at[place(0), 0]}
     for t in (2, 0, 1):
-        send(own[t], block(t, NZ - 1, 0), ring_s.at[t, 0, 0], ring_r.at[t, NZ - 1], zp)
-        send(own[t], block(t, 1, 0), ring_s.at[t, 1, 0], ring_r.at[t, 1], zm)
-        send(own[t], block(t, 0, 1), sib_s.at[t, 0], sib_r.at[t, 0], sib)
+        send(mine_of[t], block(t, NZ - 1, 0), ring_s.at[t, 0, 0], ring_r.at[t, NZ - 1], zp)
+        send(mine_of[t], block(t, 1, 0), ring_s.at[t, 1, 0], ring_r.at[t, 1], zm)
+        send(mine_of[t], block(t, 0, 1), sib_s.at[t, 0], sib_r.at[t, 0], sib)
 
     def hop(k, tensors):
         for t in tensors:
@@ -168,7 +168,7 @@
             for l in range(L):
                 slots[l, i * PAIR : (i + 1) * PAIR, :] = got[l * PAIR : (l + 1) * PAIR]
 
-    def experts(i0, i1):
+    def inner(i0, i1):
         r0, r1 = i0 * PAIR, i1 * PAIR
 
         def body(l, carry):
@@ -185,8 +185,16 @@
             d_gate = d_hidden * u * s * (1.0 + g * (1.0 - s))
             d_proj = jnp.concatenate([d_gate, d_hidden * gs], axis=1).astype(BF16)
             DP[l, r0:r1] = d_proj
-            out = dot(hidden, down_w, (1, 1)).astype(BF16)
-            back = dot(d_proj, up_w, (1, 1)).astype(BF16)
+            return carry
+
+        lax.fori_loop(0, L, body, 0)
+
+    def outer(i0, i1):
+        r0, r1 = i0 * PAIR, i1 * PAIR
+
+        def body(l, carry):
+            out = dot(GH[l, r0:r1], W[l, :, :, :, F:W3].reshape(D, H), (1, 1)).astype(BF16)
+            back = dot(DP[l, r0:r1], W[l, :, :, :, 0:F].reshape(D, F), (1, 1)).astype(BF16)
             at = pl.ds(pl.multiple_of(l * PAIR, 16), PAIR)
             for i in range(i0, i1):
                 part = slice((i - i0) * PAIR, (i - i0 + 1) * PAIR)
@@ -219,30 +227,35 @@
     hop(1, (1,))
     for distance in (0, 1, 7):
         dispatch(distance)
-    experts(0, 3)
     hop(2, (2, 0))
     hop(2, (1,))
     dispatch(2)
     dispatch(6)
-    experts(3, 5)
-    combine(0, 3)
+    inner(0, 5)
+    outer(0, 5)
     hop(3, (2, 0))
     hop(3, (1,))
+    combine(0, 5)
     dispatch(3)
     dispatch(5)
-    experts(5, 7)
-    combine(3, 5)
     hop(4, (2, 0, 1))
     dispatch(4)
-    experts(7, 8)
-
-    def gradient(l, q):
+    inner(5, 8)
+
+    def own(l):
+        return Q.at[l // 2] if l % 2 == 0 else W.at[l]
+
+    def gradient(l):
+        own(l)[:, :, :, 0:F] = dot(Xs[l], DP[l], (0, 0)).astype(BF16).reshape(NX, NX, 64, F)
+        own(l)[:, :, :, F:W3] = dot(Cs[l], GH[l], (0, 0)).astype(BF16).reshape(NX, NX, 64, H)
+
+    def gradient_piece(l, q):
         columns = pl.ds(pl.multiple_of(q * 256, 256), 256)
-        W[l, q, :, :, 0:F] = dot(Xs[l, :, columns], DP[l], (0, 0)).astype(BF16).reshape(NX, 64, F)
-        W[l, q, :, :, F:W3] = dot(Cs[l, :, columns], GH[l], (0, 0)).astype(BF16).reshape(NX, 64, H)
-
-    def chunk(h, l, q, n):
-        return (l, n, q) if h == 0 else (l, q, n)
+        own(l)[q, :, :, 0:F] = dot(Xs[l, :, columns], DP[l], (0, 0)).astype(BF16).reshape(NX, 64, F)
+        own(l)[q, :, :, F:W3] = dot(Cs[l, :, columns], GH[l], (0, 0)).astype(BF16).reshape(NX, 64, H)
+
+    def chunk(h, q, n):
+        return (n, q) if h == 0 else (q, n)
 
     def axes(h, stage):
         along_x = (h == 0) == (stage == 1)
@@ -255,21 +268,21 @@
         at, plus, minus = axes(h, 1)
         n = second(h, o)
         send(
-            W.at[chunk(h, 2 * h + way, (at + 2) % NX, n)], fwd1.at[h, way, n],
+            own(2 * h + way).at[chunk(h, (at + 2) % NX, n)], fwd1.at[h, way, n],
             x1_s.at[h, way, o], x1_r.at[h, way, o], (plus, minus)[way],
         )
 
     def near1(h, way):
         at, plus, minus = axes(h, 1)
         l, q = 2 * h + 1 - way, (at + (1, 3)[way]) % NX
-        source = W.at[l, :, q] if h == 0 else W.at[l, q]
+        source = own(l).at[:, q] if h == 0 else own(l).at[q]
         send(source, fin1.at[h, way, 1 - way], x1_s.at[h, way, 4], x1_r.at[h, way, 4], (plus, minus)[way])
 
     def relay1(h, way, o):
         at, plus, minus = axes(h, 1)
         n = second(h, o)
         arrived(fwd1.at[h, way, n], x1_r.at[h, way, o])
-        mine = W[chunk(h, 2 * h + way, (at + (1, 3)[way]) % NX, n)]
+        mine = own(2 * h + way)[chunk(h, (at + (1, 3)[way]) % NX, n)]
         fwd1[h, way, n] = (fwd1[h, way, n].astype(F32) + mine.astype(F32)).astype(BF16)
         send(
             fwd1.at[h, way, n], fin1.at[h, way, way, n],
@@ -284,29 +297,29 @@
                 arrived(fin1.at[h, way, 1 - way], x1_r.at[h, way, 4])
             arrived(fin1.at[h, way, way, n], x1_r.at[h, way, 5 + o])
         for slot in range(2):
-            own = chunk(h, 2 * h + slot, at, n)
-            total = W[own].astype(F32) + fin1[h, 0, slot, n].astype(F32) + fin1[h, 1, slot, n].astype(F32)
-            W[own] = total.astype(BF16)
+            held_ref, index = own(2 * h + slot), chunk(h, at, n)
+            total = held_ref[index].astype(F32) + fin1[h, 0, slot, n].astype(F32) + fin1[h, 1, slot, n].astype(F32)
+            held_ref[index] = total.astype(BF16)
 
     def held(h, l, q):
-        return chunk(h, l, axes(h, 1)[0], q)
+        return own(l).at[chunk(h, axes(h, 1)[0], q)]
 
     def far2(h):
         for way in range(2):
             send(
-                W.at[held(h, 2 * h + way, second(h, 2))], fwd2.at[h, way],
+                held(h, 2 * h + way, second(h, 2)), fwd2.at[h, way],
                 x2_s.at[h, way, 0], x2_r.at[h, way, 0], axes(h, 2)[1 + way],
             )
 
     def near2(h, way):
         send(
-            W.at[held(h, 2 * h + 1 - way, second(h, (1, 3)[way]))], fin2.at[h, way, 1 - way],
+            held(h, 2 * h + 1 - way, second(h, (1, 3)[way])), fin2.at[h, way, 1 - way],
             x2_s.at[h, way, 1], x2_r.at[h, way, 1], axes(h, 2)[1 + way],
         )
 
     def relay2(h, way):
         arrived(fwd2.at[h, way], x2_r.at[h, way, 0])
-        mine = W[held(h, 2 * h + way, second(h, (1, 3)[way]))]
+        mine = held(h, 2 * h + way, second(h, (1, 3)[way]))[...]
         fwd2[h, way] = (fwd2[h, way].astype(F32) + mine.astype(F32)).astype(BF16)
         send(fwd2.at[h, way], fin2.at[h, way, way], x2_s.at[h, way, 2], x2_r.at[h, way, 2], axes(h, 2)[1 + way])
 
@@ -316,7 +329,7 @@
             arrived(fin2.at[h, way, way], x2_r.at[h, way, 2])
         for slot in range(2):
             l = 2 * h + slot
-            total = W[l, yy, xx].astype(F32) + fin2[h, 0, slot].astype(F32) + fin2[h, 1, slot].astype(F32)
+            total = own(l)[yy, xx].astype(F32) + fin2[h, 0, slot].astype(F32) + fin2[h, 1, slot].astype(F32)
             fs[l] = total.astype(BF16)
 
     def total_of(parts):
@@ -334,89 +347,91 @@
 
     HALF = TOK // 2
 
-    def reduce_step(j):
-        for part in range(2):
-            rows = slice(part * HALF, (part + 1) * HALF)
-            span = pl.ds(part * HALF, HALF)
-            for t, way, targets, slots, peer in ways:
-                if j >= len(targets):
-                    continue
-                i = place(targets[j])
-                mine, other = ((xg, sibo), (cg, sibg))[t]
-                if part == 0:
-                    arrived(other.at[i], rsib_r.at[t, i])
-                parts = [mine[i, rows, :], other[i, rows, :]]
-                if j > 0:
-                    arrived(slots.at[j - 1, span], rz_r.at[t, way, j - 1, part])
-                    parts.append(slots[j - 1, rows, :])
-                mine[i, rows, :] = total_of(parts)
-                send(mine.at[i, span], slots.at[j, span], rz_s.at[t, way, j, part], rz_r.at[t, way, j, part], peer)
-
-    def reduce_end():
+    def reduce_step(j, part):
+        rows = slice(part * HALF, (part + 1) * HALF)
+        span = pl.ds(part * HALF, HALF)
+        for t, way, targets, slots, peer in ways:
+            if j >= len(targets):
+                continue
+            i = place(targets[j])
+            mine, other = ((xg, sibo), (cg, sibg))[t]
+            if part == 0:
+                arrived(other.at[i], rsib_r.at[t, i])
+            parts = [mine[i, rows, :], other[i, rows, :]]
+            if j > 0:
+                arrived(slots.at[j - 1, span], rz_r.at[t, way, j - 1, part])
+                parts.append(slots[j - 1, rows, :])
+            mine[i, rows, :] = total_of(parts)
+            send(mine.at[i, span], slots.at[j, span], rz_s.at[t, way, j, part], rz_r.at[t, way, j, part], peer)
+
+    def reduce_end(part):
         i = place(0)
-        for part in range(2):
-            rows = slice(part * HALF, (part + 1) * HALF)
-            span = pl.ds(part * HALF, HALF)
-            for t, mine, other, plus, minus, out in ((0, xg, sibo, rlp, rlm, lo_ref), (1, cg, sibg, rgp, rgm, go_ref)):
-                np_, nm = (3, 2) if t == 0 else (2, 3)
-                if part == 0:
-                    arrived(other.at[i], rsib_r.at[t, i])
-                arrived(plus.at[np_, span], rz_r.at[t, 0, np_, part])
-                arrived(minus.at[nm, span], rz_r.at[t, 1, nm, part])
-                out[rows, :] = total_of([mine[i, rows, :], other[i, rows, :], plus[np_, rows, :], minus[nm, rows, :]])
-
-    def gradients(h, way, o):
-        gradient(2 * h + way, (yy + o) % NX)
-
-    for way in range(2):
-        gradients(0, way, 2)
-        far1(0, way, 2)
-    for way in range(2):
-        gradients(1, way, 2)
-        for o in (2, 1, 3, 0):
-            far1(1, way, o)
+        rows = slice(part * HALF, (part + 1) * HALF)
+        span = pl.ds(part * HALF, HALF)
+        for t, mine, other, plus, minus, out in ((0, xg, sibo, rlp, rlm, lo_ref), (1, cg, sibg, rgp, rgm, go_ref)):
+            np_, nm = (3, 2) if t == 0 else (2, 3)
+            if part == 0:
+                arrived(other.at[i], rsib_r.at[t, i])
+            arrived(plus.at[np_, span], rz_r.at[t, 0, np_, part])
+            arrived(minus.at[nm, span], rz_r.at[t, 1, nm, part])
+            out[rows, :] = total_of([mine[i, rows, :], other[i, rows, :], plus[np_, rows, :], minus[nm, rows, :]])
+
+    gradient(0)
+    for o in (2, 1, 3, 0):
+        far1(0, 0, o)
+    near1(0, 1)
+    gradient_piece(2, (yy + 2) % NX)
+    for o in (2, 1, 3, 0):
+        far1(1, 0, o)
+    gradient_piece(2, (yy + 3) % NX)
+    near1(1, 1)
+    outer(5, 8)
     combine(7, 8)
     combine(5, 7)
-    for way in range(2):
-        gradients(0, way, 1)
-        far1(0, way, 1)
-    reduce_step(0)
-    for o in (3, 0):
-        for way in range(2):
-            gradients(0, way, o)
-            far1(0, way, o)
+    gradient(1)
+    for o in (2, 1, 3, 0):
+        far1(0, 1, o)
     near1(0, 0)
-    near1(0, 1)
-    gradients(1, 1, 1)
+    reduce_step(0, 0)
+    reduce_step(0, 1)
+    gradient_piece(2, (yy + 1) % NX)
+    gradient_piece(2, yy)
+    gradient(3)
+    for o in (2, 1, 3, 0):
+        far1(1, 1, o)
     near1(1, 0)
-    gradients(1, 0, 3)
-    near1(1, 1)
-    gradients(1, 0, 1)
-    gradients(1, 1, 3)
-    gradients(1, 0, 0)
-    gradients(1, 1, 0)
-    reduce_step(1)
-    for o in (2, 1, 3, 0):
+    for h in range(2):
+        for o in (2, 1, 3, 0):
+            relay1(h, 0, o)
+    reduce_step(1, 0)
+    for h in range(2):
+        relay1(h, 1, 2)
+    reduce_step(1, 1)
+    for o in (1, 3):
         for h in range(2):
-            for way in range(2):
-                relay1(h, way, o)
-    reduce_step(2)
+            relay1(h, 1, o)
+    reduce_step(2, 0)
+    for h in range(2):
+        relay1(h, 1, 0)
     for h in range(2):
         settle1(h, 2)
         far2(h)
-    reduce_step(3)
+    reduce_step(2, 1)
     for o, way in ((1, 0), (3, 1)):
         for h in range(2):
             settle1(h, o)
             near2(h, way)
+    reduce_step(3, 0)
+    for h in range(2):
+        settle1(h, 0)
     for h in range(2):
         for way in range(2):
             relay2(h, way)
-    settle1(0, 0)
-    settle1(1, 0)
-    reduce_end()
+    reduce_step(3, 1)
+    reduce_end(0)
     settle2(0)
     settle2(1)
+    reduce_end(1)
     ogu_ref[...] = jnp.swapaxes(fs[:, :, 0:F], 0, 1)
     odn_ref[...] = jnp.swapaxes(fs[:, :, F:W3], 0, 1)
     for copy in sends:
@@ -445,6 +460,7 @@
         out_specs=(vmem, vmem, vmem, vmem),
         scratch_shapes=[
             pltpu.VMEM((L, NX, NX, rows, W3), BF16),
+            pltpu.VMEM((2, NX, NX, rows, W3), BF16),
             pltpu.VMEM((256, L, F), BF16),
             pltpu.VMEM((256, L, H), BF16),
             pltpu.VMEM((NZ, 2 * TOK, D), BF16),

time: 123 us -> 116 us (0.943)
  Pallas kernels: 122 us -> 115 us
    pallas_call x1, Pallas kernels: 120 us -> 113 us  [per_device(): pl.pallas_call(kernel, out_shape=(jax.ShapeDtypeStruct((TOK, D), BF16), j...]
where the time goes in v3:
time: 116 us
  Pallas kernels  115 us (99%)
    pallas_call x1, Pallas kernels, per_device(): pl.pallas_call(kernel, out_shape=(jax.ShapeDtypeStruct((TOK, D), BF16), j...  113 us

profile of v3, /device:TPU:1, one launch (start us, length us, event | category | flops | bytes accessed | tf_op | source)
XLA Modules:
  0.0 116.1 jit_solution(9844912146626120512)
XLA Ops:
  0.6 113.3 %shard_map.93 = (bf16[128,1024]{1,0:T(8,128)(2,1)}, bf16[128,1024]{1,0:T(8,128)(2,1)}, bf16[64,4,768]{2,1,0:T(4,128)(2,1)}, bf16[64,4,384]{2,1,0:T(4,128)(2,1)}) custom-call(bf16[128,1024]{1,0:T(8,128)(2,1)} %x_hbm.1, s32[8,128]{1,0:T(8,128)} %bitcast.2, f32[8,128]{1,0:T(8,128)} %bitcast.3, bf16[128,1024]{1,0:T(8,128)(2,1)} %c_hbm.1, ...), custom_call_target="tpu_custom_call" | custom-call | tf_op jit(solution)/shard_map/pallas_call | solution.py:451
  113.9 2.2 %shard_map.94 = (bf16[128,1024]{1,0:T(8,128)(2,1)}, bf16[128,1024]{1,0:T(8,128)(2,1)}, bf16[64,4,768]{2,1,0:T(4,128)(2,1)}, bf16[64,4,384]{2,1,0:T(4,128)(2,1)}) custom-call(bf16[128,1024]{1,0:T(8,128)(2,1)} %get-tuple-element.8.refs_0_, bf16[128,1024]{1,0:T(8,128)(2,1)} %get-tuple-element.9.refs_1_, bf16[64,4,768]{2,1,0:T(4,128)(2,1)} %get-tuple-element.10.refs_2_, ...), custom_call_target="tpu_custom_call" | custom-call | tf_op jit(solution)/shard_map/pallas_call | solution.py:497

commit v4 on v3

--- a/solution.py
+++ b/solution.py
@@ -168,7 +168,7 @@
             for l in range(L):
                 slots[l, i * PAIR : (i + 1) * PAIR, :] = got[l * PAIR : (l + 1) * PAIR]
 
-    def inner(i0, i1):
+    def inner(i0, i1, l0=0, l1=L):
         r0, r1 = i0 * PAIR, i1 * PAIR
 
         def body(l, carry):
@@ -187,7 +187,7 @@
             DP[l, r0:r1] = d_proj
             return carry
 
-        lax.fori_loop(0, L, body, 0)
+        lax.fori_loop(l0, l1, body, 0)
 
     def outer(i0, i1):
         r0, r1 = i0 * PAIR, i1 * PAIR
@@ -240,7 +240,6 @@
     dispatch(5)
     hop(4, (2, 0, 1))
     dispatch(4)
-    inner(5, 8)
 
     def own(l):
         return Q.at[l // 2] if l % 2 == 0 else W.at[l]
@@ -376,30 +375,34 @@
             arrived(minus.at[nm, span], rz_r.at[t, 1, nm, part])
             out[rows, :] = total_of([mine[i, rows, :], other[i, rows, :], plus[np_, rows, :], minus[nm, rows, :]])
 
+    inner(5, 8, 0, 1)
     gradient(0)
     for o in (2, 1, 3, 0):
         far1(0, 0, o)
     near1(0, 1)
+    inner(5, 8, 2, 3)
     gradient_piece(2, (yy + 2) % NX)
     for o in (2, 1, 3, 0):
         far1(1, 0, o)
     gradient_piece(2, (yy + 3) % NX)
     near1(1, 1)
+    inner(5, 8, 1, 2)
+    inner(5, 8, 3, 4)
     outer(5, 8)
     combine(7, 8)
     combine(5, 7)
+    reduce_step(0, 0)
+    reduce_step(0, 1)
     gradient(1)
     for o in (2, 1, 3, 0):
         far1(0, 1, o)
     near1(0, 0)
-    reduce_step(0, 0)
-    reduce_step(0, 1)
-    gradient_piece(2, (yy + 1) % NX)
-    gradient_piece(2, yy)
     gradient(3)
     for o in (2, 1, 3, 0):
         far1(1, 1, o)
     near1(1, 0)
+    gradient_piece(2, (yy + 1) % NX)
+    gradient_piece(2, yy)
     for h in range(2):
         for o in (2, 1, 3, 0):
             relay1(h, 0, o)

time: 116 us -> 115 us (level)
    pallas_call x1, Pallas kernels: 113 us -> 112 us  [per_device(): pl.pallas_call(kernel, out_shape=(jax.ShapeDtypeStruct((TOK, D), BF16), j...]
where the time goes in v4:
time: 115 us
  Pallas kernels  114 us (99%)
    pallas_call x1, Pallas kernels, per_device(): pl.pallas_call(kernel, out_shape=(jax.ShapeDtypeStruct((TOK, D), BF16), j...  112 us

profile of v4, /device:TPU:1, one launch (start us, length us, event | category | flops | bytes accessed | tf_op | source)
XLA Modules:
  0.0 114.6 jit_solution(14784587081629547073)
XLA Ops:
  0.6 111.8 %shard_map.93 = (bf16[128,1024]{1,0:T(8,128)(2,1)}, bf16[128,1024]{1,0:T(8,128)(2,1)}, bf16[64,4,768]{2,1,0:T(4,128)(2,1)}, bf16[64,4,384]{2,1,0:T(4,128)(2,1)}) custom-call(bf16[128,1024]{1,0:T(8,128)(2,1)} %x_hbm.1, s32[8,128]{1,0:T(8,128)} %bitcast.2, f32[8,128]{1,0:T(8,128)} %bitcast.3, bf16[128,1024]{1,0:T(8,128)(2,1)} %c_hbm.1, ...), custom_call_target="tpu_custom_call" | custom-call | tf_op jit(solution)/shard_map/pallas_call | solution.py:454
  112.4 2.2 %shard_map.94 = (bf16[128,1024]{1,0:T(8,128)(2,1)}, bf16[128,1024]{1,0:T(8,128)(2,1)}, bf16[64,4,768]{2,1,0:T(4,128)(2,1)}, bf16[64,4,384]{2,1,0:T(4,128)(2,1)}) custom-call(bf16[128,1024]{1,0:T(8,128)(2,1)} %get-tuple-element.8.refs_0_, bf16[128,1024]{1,0:T(8,128)(2,1)} %get-tuple-element.9.refs_1_, bf16[64,4,768]{2,1,0:T(4,128)(2,1)} %get-tuple-element.10.refs_2_, ...), custom_call_target="tpu_custom_call" | custom-call | tf_op jit(solution)/shard_map/pallas_call | solution.py:500

commit v5 on v4

--- a/solution.py
+++ b/solution.py
@@ -219,6 +219,29 @@
             send(xg.at[i, pl.ds(TOK, TOK)], sibo.at[i], rsib_s.at[0, i], rsib_r.at[0, i], sib)
             send(cg.at[i, pl.ds(TOK, TOK)], sibg.at[i], rsib_s.at[1, i], rsib_r.at[1, i], sib)
 
+    EARLY = 5 * PAIR
+
+    def own(l):
+        return Q.at[l // 2] if l % 2 == 0 else W.at[l]
+
+    def early(l):
+        own(l)[:, :, :, 0:F] = dot(Xs[l, 0:EARLY], DP[l, 0:EARLY], (0, 0)).astype(BF16).reshape(NX, NX, 64, F)
+        own(l)[:, :, :, F:W3] = dot(Cs[l, 0:EARLY], GH[l, 0:EARLY], (0, 0)).astype(BF16).reshape(NX, NX, 64, H)
+
+    def gradient(l):
+        for slots, units, first, last in ((Xs, DP, 0, F), (Cs, GH, F, W3)):
+            start = EARLY if l % 2 == 0 else 0
+            term = dot(slots[l, start:SLOTS], units[l, start:SLOTS], (0, 0)).reshape(NX, NX, 64, last - first)
+            if l % 2 == 0:
+                term = term + own(l)[:, :, :, first:last].astype(F32)
+            own(l)[:, :, :, first:last] = term.astype(BF16)
+
+    def gradient_piece(l, q):
+        columns = pl.ds(pl.multiple_of(q * 256, 256), 256)
+        for slots, units, first, last in ((Xs, DP, 0, F), (Cs, GH, F, W3)):
+            term = dot(slots[l, EARLY:SLOTS, columns], units[l, EARLY:SLOTS], (0, 0)).reshape(NX, 64, last - first)
+            own(l)[q, :, :, first:last] = (term + own(l)[q, :, :, first:last].astype(F32)).astype(BF16)
+
     for group in range(NX):
         relayout(group)
     for copy in own_copies:
@@ -234,24 +257,14 @@
     inner(0, 5)
     outer(0, 5)
     hop(3, (2, 0))
+    early(0)
+    early(2)
     hop(3, (1,))
     combine(0, 5)
     dispatch(3)
     dispatch(5)
     hop(4, (2, 0, 1))
     dispatch(4)
-
-    def own(l):
-        return Q.at[l // 2] if l % 2 == 0 else W.at[l]
-
-    def gradient(l):
-        own(l)[:, :, :, 0:F] = dot(Xs[l], DP[l], (0, 0)).astype(BF16).reshape(NX, NX, 64, F)
-        own(l)[:, :, :, F:W3] = dot(Cs[l], GH[l], (0, 0)).astype(BF16).reshape(NX, NX, 64, H)
-
-    def gradient_piece(l, q):
-        columns = pl.ds(pl.multiple_of(q * 256, 256), 256)
-        own(l)[q, :, :, 0:F] = dot(Xs[l, :, columns], DP[l], (0, 0)).astype(BF16).reshape(NX, 64, F)
-        own(l)[q, :, :, F:W3] = dot(Cs[l, :, columns], GH[l], (0, 0)).astype(BF16).reshape(NX, 64, H)
 
     def chunk(h, q, n):
         return (n, q) if h == 0 else (q, n)

time: 115 us -> 115 us (level)
  no operation moved by 1% of the time
where the time goes in v5:
time: 115 us
  Pallas kernels  114 us (99%)
    pallas_call x1, Pallas kernels, per_device(): pl.pallas_call(kernel, out_shape=(jax.ShapeDtypeStruct((TOK, D), BF16), j...  112 us

profile of v5, /device:TPU:1, one launch (start us, length us, event | category | flops | bytes accessed | tf_op | source)
XLA Modules:
  0.0 114.6 jit_solution(2814209726409153348)
XLA Ops:
  0.6 111.8 %shard_map.93 = (bf16[128,1024]{1,0:T(8,128)(2,1)}, bf16[128,1024]{1,0:T(8,128)(2,1)}, bf16[64,4,768]{2,1,0:T(4,128)(2,1)}, bf16[64,4,384]{2,1,0:T(4,128)(2,1)}) custom-call(bf16[128,1024]{1,0:T(8,128)(2,1)} %x_hbm.1, s32[8,128]{1,0:T(8,128)} %bitcast.2, f32[8,128]{1,0:T(8,128)} %bitcast.3, bf16[128,1024]{1,0:T(8,128)(2,1)} %c_hbm.1, ...), custom_call_target="tpu_custom_call" | custom-call | tf_op jit(solution)/shard_map/pallas_call | solution.py:467
  112.4 2.2 %shard_map.94 = (bf16[128,1024]{1,0:T(8,128)(2,1)}, bf16[128,1024]{1,0:T(8,128)(2,1)}, bf16[64,4,768]{2,1,0:T(4,128)(2,1)}, bf16[64,4,384]{2,1,0:T(4,128)(2,1)}) custom-call(bf16[128,1024]{1,0:T(8,128)(2,1)} %get-tuple-element.8.refs_0_, bf16[128,1024]{1,0:T(8,128)(2,1)} %get-tuple-element.9.refs_1_, bf16[64,4,768]{2,1,0:T(4,128)(2,1)} %get-tuple-element.10.refs_2_, ...), custom_call_target="tpu_custom_call" | custom-call | tf_op jit(solution)/shard_map/pallas_call | solution.py:513
